TPU v7x, 256 devices: a whole 4x4x8 slice. The times are simulated.
256 devices in a mesh: group: 4 (over x), sub: 64 (over z, y, core).
Axes of the slice: x: 4, y: 4, z: 8, core: 2. Of those that a mesh axis runs over, the one named last changes fastest.
Arguments:
- load_cases: bfloat16 [4, 64, 1536, 256], P('group', 'sub'), may hold values from -6 to 6
- inv_schur: bfloat16 [4, 64, 1536, 1536], P('group', 'sub'), may hold values from -0.15625 to 0.15625
- schur_blocks: bfloat16 [4, 64, 1536, 1536], P('group', 'sub'), may hold values from -0.15625 to 0.15625
- coarse_basis: float32 [4, 64, 1536], P('group', 'sub'), may hold values from -0.53033006 to 0.53033006
- coarse_map: int32 [4, 64, 12], P('group', 'sub'), may hold values from 0 to 1023
- multiplicity: int32 [4, 64, 12], P('group', 'sub'), may hold values from 2 to 4
- recv_code: int32 [4, 64, 12], P('group', 'sub'), may hold values from 0 to 23, as said below
- send_blocks: int32 [4, 64, 24], P('group', 'sub'), may hold values from -1 to 11, as said below
- coarse_inv: float32 [4, 1024, 1024], P('group', 'sub'), may hold values from -0.1875 to 0.1875
Outputs:
- multipliers: float32 [4, 64, 1536, 256], P('group', 'sub')
Inputs may be any that keep to these rules, and one draw needn't show every extreme that they name: `recv_code`: within one subdomain the blocks read distinct codes; in every subdomain all 4 slots of one direction are read. `send_blocks`: entry d * 4 + j is the block a subdomain sends as slot j of direction d, to the subdomain that reads direction d from it; it is -1 exactly where that subdomain reads nothing from the slot.
All inputs are finite; a program needn't handle non-finite values.
Results may differ from a plain program's by a relative error of at most 0.0085.
Values may be sent and summed in bfloat16 or wider, within the bound.
A program may use at most 64 MiB of HBM per device.

v0:
```python
import jax
import jax.numpy as jnp
from jax import lax
from jax.sharding import PartitionSpec as P

BLK = 128
DIRS = 6
CAP = 4
ITERS = 2


OFFSETS = (1, -1, 2, -2, 1, -1)


def passed_along(block, axis, distance):
    devices = range(lax.axis_size(axis))
    route = [((i - distance) % len(devices), i) for i in devices]
    return lax.ppermute(block, axis, route)


def joined_along(parts, dim):
    dims = list(parts.shape[1:])
    dims[dim] *= parts.shape[0]
    return jnp.moveaxis(parts, 0, dim).reshape(dims)


def from_everyone(x, axis):
    peers = lax.axis_size(axis)
    return lax.all_to_all(jnp.broadcast_to(x[None], (peers, *x.shape)), axis, 0, 0, tiled=True)


def gather_directly(x, axis, dim):
    return joined_along(from_everyone(x, axis), dim)


def jump(values, read_codes, outgoing):
    block_count, block_size, case_count = values.shape
    picked = jnp.take(values, jnp.maximum(outgoing, 0), axis=0)
    picked = jnp.where((outgoing >= 0)[:, None, None], picked, jnp.zeros((), jnp.bfloat16))
    send_slabs = picked.reshape(DIRS, CAP, block_size, case_count)
    arrived = []
    for direction in range(4):
        arrived.append(passed_along(send_slabs[direction], "sub", OFFSETS[direction]))
    for direction in (4, 5):
        arrived.append(passed_along(send_slabs[direction], "group", OFFSETS[direction]))
    received = jnp.stack(arrived).reshape(DIRS * CAP, block_size, case_count)
    remote = jnp.take(received, read_codes, axis=0)
    return values.astype(jnp.float32) - remote.astype(jnp.float32)


def on_device(
    load_cases,
    inv_schur,
    schur_blocks,
    coarse_basis,
    coarse_map,
    multiplicity,
    recv_code,
    send_blocks,
    coarse_inv,
):
    dof_count = inv_schur.shape[2]
    case_count = load_cases.shape[3]
    block_count = dof_count // BLK
    solve_matrix = inv_schur[0, 0]
    dirichlet_matrix = schur_blocks[0, 0]
    basis_rows = coarse_basis[0, 0].reshape(block_count, BLK)
    read_codes = recv_code[0, 0]
    outgoing = send_blocks[0, 0]
    weights = (1.0 / multiplicity[0, 0].astype(jnp.float32))[:, None, None]
    own_rows = coarse_inv[0]
    own_map = coarse_map[0, 0]
    every_map = gather_directly(own_map, "sub", 0)
    wanted_columns = jnp.take(own_rows, every_map, axis=1)
    my_columns = lax.all_to_all(
        wanted_columns.astype(jnp.bfloat16), "sub", split_axis=1, concat_axis=0, tiled=True
    ).astype(wanted_columns.dtype)
    column_rows = jnp.take(my_columns, every_map, axis=0)
    multipliers = jnp.zeros((dof_count, case_count), jnp.float32)
    for iteration in range(ITERS):
        residual_load = (load_cases[0, 0].astype(jnp.float32) - multipliers).astype(jnp.bfloat16)
        displacement = jnp.dot(
            solve_matrix, residual_load, preferred_element_type=jnp.float32
        ).reshape(block_count, BLK, case_count)
        projected = jnp.sum(basis_rows[:, :, None] * displacement, axis=1)
        every_projected = gather_directly(projected, "sub", 0)
        coarse_here = jnp.einsum("nb,nc->bc", column_rows, every_projected)
        corrected = (displacement + basis_rows[:, :, None] * coarse_here[:, None, :]).astype(
            jnp.bfloat16
        )
        scaled = (jump(corrected, read_codes, outgoing) * weights).astype(jnp.bfloat16)
        dirichlet = jnp.dot(
            dirichlet_matrix,
            scaled.reshape(dof_count, case_count),
            preferred_element_type=jnp.float32,
        ).reshape(block_count, BLK, case_count)
        dual_step = (dirichlet * weights).astype(jnp.bfloat16)
        multipliers = multipliers + jump(dual_step, read_codes, outgoing).reshape(
            dof_count, case_count
        )
    return multipliers[None, None]


def solution(mesh):
    placed = (
        P("group", "sub", None, None),
        P("group", "sub", None, None),
        P("group", "sub", None, None),
        P("group", "sub", None),
        P("group", "sub", None),
        P("group", "sub", None),
        P("group", "sub", None),
        P("group", "sub", None),
        P("group", "sub", None),
    )
    return jax.shard_map(
        on_device,
        mesh=mesh,
        in_specs=placed,
        out_specs=P("group", "sub", None, None),
        check_vma=False,
    )
```

profile of v0, /device:TPU:6, one launch (start us, length us, event | category | flops | bytes accessed | tf_op | source)
XLA Modules:
  0.0 245.2 jit_solution(1981972805027480971)
XLA Ops:
  1.3 12.1 %all-to-all-start = ((s32[64,1,12]{2,1,0:T(1,128)}), s32[64,1,12]{2,1,0:T(1,128)S(1)}, u32[]{:S(2)}, u32[]{:S(2)}) async-start(s32[64,1,12]{2,1,0:T(1,128)} %broadcast_in_dim.87), calls=%async_computation | async-start | bytes 65536 | tf_op jit(solution)/shard_map/all_to_all | solution.py:29
  14.1 4.0 %multiply_reduce_fusion.1 = (bf16[12,256]{1,0:T(8,128)(2,1)S(1)}, f32[12,128,256]{2,1,0:T(8,128)S(1)}) fusion(f32[12,128]{1,0:T(8,128)S(1)} %bitcast.135, bf16[12,128,1536]{2,1,0:T(8,128)(2,1)} %bitcast.143, bf16[1,1,1536,256]{3,2,1,0:T(8,128)(2,1)} %param.13), kind=kOutput, calls=%fused_computation.34 | convolution fusion | flops 1208742912 | bytes 7090176 | tf_op jit(solution)/shard_map/dot_general | solution.py:82
  18.3 4.6 %all-to-all-done = s32[64,1,12]{2,1,0:T(1,128)S(1)} async-done(((s32[64,1,12]{2,1,0:T(1,128)}), s32[64,1,12]{2,1,0:T(1,128)S(1)}, u32[]{:S(2)}, u32[]{:S(2)}) %all-to-all-start) | async-done | bytes 3104 | tf_op jit(solution)/shard_map/all_to_all | solution.py:29
  23.2 1.9 gather_fusion
  26.4 5.7 %all-to-all-start.1 = ((bf16[16,64,12]{2,0,1:T(8,128)(2,1)}), bf16[16,64,12]{2,0,1:T(8,128)(2,1)S(1)}, u32[]{:S(2)}, u32[]{:S(2)}) async-start(bf16[16,64,12]{2,0,1:T(8,128)(2,1)} %copy.31), calls=%async_computation.1 | async-start | bytes 524288 | tf_op jit(solution)/shard_map/all_to_all | solution.py:75
  32.1 12.9 %all-to-all-done.1 = bf16[16,64,12]{2,0,1:T(8,128)(2,1)S(1)} async-done(((bf16[16,64,12]{2,0,1:T(8,128)(2,1)}), bf16[16,64,12]{2,0,1:T(8,128)(2,1)S(1)}, u32[]{:S(2)}, u32[]{:S(2)}) %all-to-all-start.1) | async-done | bytes 24608 | tf_op jit(solution)/shard_map/all_to_all | solution.py:75
  45.8 5.0 %all-to-all-start.2 = ((bf16[64,12,256]{2,1,0:T(8,128)(2,1)}), bf16[64,12,256]{2,1,0:T(8,128)(2,1)S(1)}, u32[]{:S(2)}, u32[]{:S(2)}) async-start(bf16[64,12,256]{2,1,0:T(8,128)(2,1)} %broadcast_in_dim.92), calls=%async_computation.2 | async-start | bytes 1048576 | tf_op jit(solution)/shard_map/all_to_all | solution.py:29
  52.2 1.9 gather_fusion.1
  54.1 14.3 %all-to-all-done.2 = bf16[64,12,256]{2,1,0:T(8,128)(2,1)S(1)} async-done(((bf16[64,12,256]{2,1,0:T(8,128)(2,1)}), bf16[64,12,256]{2,1,0:T(8,128)(2,1)S(1)}, u32[]{:S(2)}, u32[]{:S(2)}) %all-to-all-start.2) | async-done | bytes 393248 | tf_op jit(solution)/shard_map/all_to_all | solution.py:29
  73.3 4.7 %collective-permute-start.1 = (bf16[4,128,256]{2,1,0:T(8,128)(2,1)S(1)}, bf16[4,128,256]{2,1,0:T(8,128)(2,1)S(1)}, u32[]{:S(2)}, u32[]{:S(2)}) collective-permute-start(bf16[4,128,256]{2,1,0:T(8,128)(2,1)S(1)} %get-tuple-element.31), channel_id=1, source_target_pairs={{1,0},{2,1},{3,2},{4,3},{5,4},{6,5},{7,6},{8,7},{9,8},{10,9},{11,1... | collective-permute-start | bytes 786440 | tf_op jit(solution)/shard_map/ppermute | solution.py:18
  78.8 2.4 collective-permute-start.4
  83.6 9.1 %collective-permute-done.2 = bf16[4,128,256]{2,1,0:T(8,128)(2,1)S(1)} collective-permute-done((bf16[4,128,256]{2,1,0:T(8,128)(2,1)S(1)}, bf16[4,128,256]{2,1,0:T(8,128)(2,1)S(1)}, u32[]{:S(2)}, u32[]{:S(2)}) %collective-permute-start.2) | collective-permute-done | bytes 262176 | tf_op jit(solution)/shard_map/ppermute | solution.py:18
  93.9 2.0 gather_fusion.3
  96.4 3.8 %fusion.6 = f32[1536,256]{0,1:T(8,128)S(1)} fusion(bf16[1536,256]{1,0:T(8,128)(2,1)S(1)} %bitcast.129, bf16[1,1,1536,1536]{3,2,1,0:T(8,128)(2,1)} %param.15), kind=kOutput, calls=%fused_computation.16 | convolution fusion | flops 1207959552 | bytes 7077888 | tf_op jit(solution)/shard_map/dot_general | solution.py:92
  104.6 5.1 %collective-permute-start.7 = (bf16[4,128,256]{2,1,0:T(8,128)(2,1)S(1)}, bf16[4,128,256]{2,1,0:T(8,128)(2,1)S(1)}, u32[]{:S(2)}, u32[]{:S(2)}) collective-permute-start(bf16[4,128,256]{2,1,0:T(8,128)(2,1)S(1)} %get-tuple-element.25), channel_id=1, source_target_pairs={{1,0},{2,1},{3,2},{4,3},{5,4},{6,5},{7,6},{8,7},{9,8},{10,9},{11,1... | collective-permute-start | bytes 786440 | tf_op jit(solution)/shard_map/ppermute | solution.py:18
  109.8 3.1 %collective-permute-start.10 = (bf16[4,128,256]{2,1,0:T(8,128)(2,1)S(1)}, bf16[4,128,256]{2,1,0:T(8,128)(2,1)S(1)}, u32[]{:S(2)}, u32[]{:S(2)}) collective-permute-start(bf16[4,128,256]{2,1,0:T(8,128)(2,1)S(1)} %get-tuple-element.22), channel_id=1, source_target_pairs={{192,0},{0,64},{64,128},{128,192},{193,1},{1,65},{65,129},{129,193... | collective-permute-start | bytes 786440 | tf_op jit(solution)/shard_map/ppermute | solution.py:18
  115.0 9.0 %collective-permute-done.8 = bf16[4,128,256]{2,1,0:T(8,128)(2,1)S(1)} collective-permute-done((bf16[4,128,256]{2,1,0:T(8,128)(2,1)S(1)}, bf16[4,128,256]{2,1,0:T(8,128)(2,1)S(1)}, u32[]{:S(2)}, u32[]{:S(2)}) %collective-permute-start.8) | collective-permute-done | bytes 262176 | tf_op jit(solution)/shard_map/ppermute | solution.py:18
  125.3 2.0 gather_fusion.5
  128.2 4.9 %fusion.12 = f32[1536,256]{0,1:T(8,128)} fusion(bf16[1536,256]{1,0:T(8,128)(2,1)S(1)} %bitcast.130, bf16[1,1,1536,1536]{3,2,1,0:T(8,128)(2,1)} %param.14), kind=kOutput, calls=%fused_computation.18 | convolution fusion | flops 1207959552 | bytes 7077888 | tf_op jit(solution)/shard_map/dot_general | solution.py:82
  135.3 32.3 %all_to_all.26 = bf16[64,12,256]{2,1,0:T(8,128)(2,1)} all-to-all(bf16[64,12,256]{2,1,0:T(8,128)(2,1)S(1)} %broadcast_in_dim.95), channel_id=1, replica_groups=mesh['group'=4,'sub'=64] {'sub'}, dimensions={0} | all-to-all | bytes 786432 | tf_op jit(solution)/shard_map/all_to_all | solution.py:29
  172.1 3.0 %gather_fusion.6 = bf16[24,128,256]{2,1,0:T(8,128)(2,1)} fusion(bf16[12,128,256]{2,1,0:T(8,128)(2,1)} %add_convert_fusion, s32[1024]{0:T(1024)S(1)} %pad_clamp_fusion.1), kind=kCustom, calls=%fused_computation.3.clone | custom fusion | bytes 3145824 | tf_op jit(solution)/shard_map/jit(_take)/gather | solution.py:38
  177.1 4.9 %collective-permute-start.13 = (bf16[4,128,256]{2,1,0:T(8,128)(2,1)S(1)}, bf16[4,128,256]{2,1,0:T(8,128)(2,1)S(1)}, u32[]{:S(2)}, u32[]{:S(2)}) collective-permute-start(bf16[4,128,256]{2,1,0:T(8,128)(2,1)S(1)} %get-tuple-element.19), channel_id=1, source_target_pairs={{1,0},{2,1},{3,2},{4,3},{5,4},{6,5},{7,6},{8,7},{9,8},{10,9},{11,1... | collective-permute-start | bytes 786440 | tf_op jit(solution)/shard_map/ppermute | solution.py:18
  182.1 3.2 %collective-permute-start.16 = (bf16[4,128,256]{2,1,0:T(8,128)(2,1)S(1)}, bf16[4,128,256]{2,1,0:T(8,128)(2,1)S(1)}, u32[]{:S(2)}, u32[]{:S(2)}) collective-permute-start(bf16[4,128,256]{2,1,0:T(8,128)(2,1)S(1)} %get-tuple-element.16), channel_id=1, source_target_pairs={{192,0},{0,64},{64,128},{128,192},{193,1},{1,65},{65,129},{129,193... | collective-permute-start | bytes 786440 | tf_op jit(solution)/shard_map/ppermute | solution.py:18
  188.8 7.6 %collective-permute-done.14 = bf16[4,128,256]{2,1,0:T(8,128)(2,1)S(1)} collective-permute-done((bf16[4,128,256]{2,1,0:T(8,128)(2,1)S(1)}, bf16[4,128,256]{2,1,0:T(8,128)(2,1)S(1)}, u32[]{:S(2)}, u32[]{:S(2)}) %collective-permute-start.14) | collective-permute-done | bytes 262176 | tf_op jit(solution)/shard_map/ppermute | solution.py:18
  199.3 3.0 %gather_fusion.7 = bf16[12,128,256]{2,1,0:T(8,128)(2,1)} fusion(bf16[24,128,256]{2,1,0:T(8,128)(2,1)} %bitcast.42, s32[1024]{0:T(1024)S(1)} %pad_clamp_fusion), kind=kCustom, calls=%fused_computation.6.clone | custom fusion | bytes 1572912 | tf_op jit(solution)/shard_map/jit(_take)/gather | solution.py:47
  203.9 4.9 %fusion.9 = f32[1536,256]{0,1:T(8,128)} fusion(bf16[1536,256]{1,0:T(8,128)(2,1)S(1)} %bitcast.128, bf16[1,1,1536,1536]{3,2,1,0:T(8,128)(2,1)} %param.15), kind=kOutput, calls=%fused_computation.17 | convolution fusion | flops 1207959552 | bytes 7077888 | tf_op jit(solution)/shard_map/dot_general | solution.py:92
  211.8 3.0 %gather_fusion.8 = bf16[24,128,256]{2,1,0:T(8,128)(2,1)} fusion(bf16[12,128,256]{2,1,0:T(8,128)(2,1)} %multiply_convert_fusion, s32[1024]{0:T(1024)S(1)} %pad_clamp_fusion.1), kind=kCustom, calls=%fused_computation.4.clone | custom fusion | bytes 3145824 | tf_op jit(solution)/shard_map/jit(_take)/gather | solution.py:38
  216.7 5.1 %collective-permute-start.19 = (bf16[4,128,256]{2,1,0:T(8,128)(2,1)S(1)}, bf16[4,128,256]{2,1,0:T(8,128)(2,1)S(1)}, u32[]{:S(2)}, u32[]{:S(2)}) collective-permute-start(bf16[4,128,256]{2,1,0:T(8,128)(2,1)S(1)} %get-tuple-element.13), channel_id=1, source_target_pairs={{1,0},{2,1},{3,2},{4,3},{5,4},{6,5},{7,6},{8,7},{9,8},{10,9},{11,1... | collective-permute-start | bytes 786440 | tf_op jit(solution)/shard_map/ppermute | solution.py:18
  221.8 3.2 %collective-permute-start.22 = (bf16[4,128,256]{2,1,0:T(8,128)(2,1)S(1)}, bf16[4,128,256]{2,1,0:T(8,128)(2,1)S(1)}, u32[]{:S(2)}, u32[]{:S(2)}) collective-permute-start(bf16[4,128,256]{2,1,0:T(8,128)(2,1)S(1)} %get-tuple-element.10), channel_id=1, source_target_pairs={{192,0},{0,64},{64,128},{128,192},{193,1},{1,65},{65,129},{129,193... | collective-permute-start | bytes 786440 | tf_op jit(solution)/shard_map/ppermute | solution.py:18
  228.5 7.6 %collective-permute-done.20 = bf16[4,128,256]{2,1,0:T(8,128)(2,1)S(1)} collective-permute-done((bf16[4,128,256]{2,1,0:T(8,128)(2,1)S(1)}, bf16[4,128,256]{2,1,0:T(8,128)(2,1)S(1)}, u32[]{:S(2)}, u32[]{:S(2)}) %collective-permute-start.20) | collective-permute-done | bytes 262176 | tf_op jit(solution)/shard_map/ppermute | solution.py:18
  239.0 3.0 %gather_fusion.9 = bf16[12,128,256]{2,1,0:T(8,128)(2,1)} fusion(bf16[24,128,256]{2,1,0:T(8,128)(2,1)} %bitcast.52, s32[1024]{0:T(1024)S(1)} %pad_clamp_fusion), kind=kCustom, calls=%fused_computation.7.clone | custom fusion | bytes 1572912 | tf_op jit(solution)/shard_map/jit(_take)/gather | solution.py:47
  242.0 3.1 %subtract_add_fusion = f32[12,128,256]{2,1,0:T(8,128)} fusion(bf16[12,128,256]{2,1,0:T(8,128)(2,1)} %gather_fusion.9, pred[12]{0:T(512)(128)(4,1)S(1)} %compare_and_fusion.2, bf16[12,128,256]{2,1,0:T(8,128)(2,1)} %copy-done, f32[12,128,256]{2,1,0:T(8,128)S(1)} %bitcast.124, f32[12]{0:T(128)S(1)} %divide_bitcast_fusion, f32[12,128,256]{2,1,0:T(8,128)S(1)} %bitcast.122), kind=kLoop, calls=%fused_computation.25 | loop fusion | flops 5111808 | bytes 6291516 | tf_op jit(solution)/shard_map/add | solution.py:98
  (126 shorter events, 52.2 us)
Async XLA Ops:
  1.3 21.7 %all-to-all-start = ((s32[64,1,12]{2,1,0:T(1,128)}), s32[64,1,12]{2,1,0:T(1,128)S(1)}, u32[]{:S(2)}, u32[]{:S(2)}) async-start(s32[64,1,12]{2,1,0:T(1,128)} %broadcast_in_dim.87), calls=%async_computation | async-start | bytes 65536 | tf_op jit(solution)/shard_map/all_to_all | solution.py:29
  14.1 4.0 %copy-start.5 = (s32[1,1,24]{2,1,0:T(1,128)S(1)}, s32[1,1,24]{2,1,0:T(1,128)}, u32[]{:S(2)}) copy-start(s32[1,1,24]{2,1,0:T(1,128)} %param.20) | copy-start | bytes 292
  14.1 4.0 %copy-start.4 = (f32[1,16,1024]{2,1,0:T(8,128)S(1)}, f32[1,16,1024]{2,1,0:T(8,128)}, u32[]{:S(2)}) copy-start(f32[1,16,1024]{2,1,0:T(8,128)} %param.21) | copy-start | bytes 196612
  25.1 25.7 %copy-start.6 = (s32[1,1,12]{2,1,0:T(1,128)S(1)}, s32[1,1,12]{2,1,0:T(1,128)}, u32[]{:S(2)}) copy-start(s32[1,1,12]{2,1,0:T(1,128)} %param.19) | copy-start | bytes 148
  26.4 18.6 %all-to-all-start.1 = ((bf16[16,64,12]{2,0,1:T(8,128)(2,1)}), bf16[16,64,12]{2,0,1:T(8,128)(2,1)S(1)}, u32[]{:S(2)}, u32[]{:S(2)}) async-start(bf16[16,64,12]{2,0,1:T(8,128)(2,1)} %copy.31), calls=%async_computation.1 | async-start | bytes 524288 | tf_op jit(solution)/shard_map/all_to_all | solution.py:75
  45.8 22.6 %all-to-all-start.2 = ((bf16[64,12,256]{2,1,0:T(8,128)(2,1)}), bf16[64,12,256]{2,1,0:T(8,128)(2,1)S(1)}, u32[]{:S(2)}, u32[]{:S(2)}) async-start(bf16[64,12,256]{2,1,0:T(8,128)(2,1)} %broadcast_in_dim.92), calls=%async_computation.2 | async-start | bytes 1048576 | tf_op jit(solution)/shard_map/all_to_all | solution.py:29
  72.8 9.2 %collective-permute-start = (bf16[4,128,256]{2,1,0:T(8,128)(2,1)S(1)}, bf16[4,128,256]{2,1,0:T(8,128)(2,1)S(1)}, u32[]{:S(2)}, u32[]{:S(2)}) collective-permute-start(bf16[4,128,256]{2,1,0:T(8,128)(2,1)S(1)} %get-tuple-element.32), channel_id=1, source_target_pairs={{63,0},{0,1},{1,2},{2,3},{3,4},{4,5},{5,6},{6,7},{7,8},{8,9},{9,10... | collective-permute-start | bytes 786440 | tf_op jit(solution)/shard_map/ppermute | solution.py:18
  73.3 10.2 %collective-permute-start.1 = (bf16[4,128,256]{2,1,0:T(8,128)(2,1)S(1)}, bf16[4,128,256]{2,1,0:T(8,128)(2,1)S(1)}, u32[]{:S(2)}, u32[]{:S(2)}) collective-permute-start(bf16[4,128,256]{2,1,0:T(8,128)(2,1)S(1)} %get-tuple-element.31), channel_id=1, source_target_pairs={{1,0},{2,1},{3,2},{4,3},{5,4},{6,5},{7,6},{8,7},{9,8},{10,9},{11,1... | collective-permute-start | bytes 786440 | tf_op jit(solution)/shard_map/ppermute | solution.py:18
  78.0 14.8 %collective-permute-start.5 = (bf16[4,128,256]{2,1,0:T(8,128)(2,1)S(1)}, bf16[4,128,256]{2,1,0:T(8,128)(2,1)S(1)}, u32[]{:S(2)}, u32[]{:S(2)}) collective-permute-start(bf16[4,128,256]{2,1,0:T(8,128)(2,1)S(1)} %get-tuple-element.27), channel_id=1, source_target_pairs={{64,0},{128,64},{192,128},{0,192},{65,1},{129,65},{193,129},{1,193... | collective-permute-start | bytes 786440 | tf_op jit(solution)/shard_map/ppermute | solution.py:18
  78.8 13.9 %collective-permute-start.4 = (bf16[4,128,256]{2,1,0:T(8,128)(2,1)S(1)}, bf16[4,128,256]{2,1,0:T(8,128)(2,1)S(1)}, u32[]{:S(2)}, u32[]{:S(2)}) collective-permute-start(bf16[4,128,256]{2,1,0:T(8,128)(2,1)S(1)} %get-tuple-element.28), channel_id=1, source_target_pairs={{192,0},{0,64},{64,128},{128,192},{193,1},{1,65},{65,129},{129,193... | collective-permute-start | bytes 786440 | tf_op jit(solution)/shard_map/ppermute | solution.py:18
  81.2 11.4 %collective-permute-start.3 = (bf16[4,128,256]{2,1,0:T(8,128)(2,1)S(1)}, bf16[4,128,256]{2,1,0:T(8,128)(2,1)S(1)}, u32[]{:S(2)}, u32[]{:S(2)}) collective-permute-start(bf16[4,128,256]{2,1,0:T(8,128)(2,1)S(1)} %get-tuple-element.29), channel_id=1, source_target_pairs={{2,0},{3,1},{4,2},{5,3},{6,4},{7,5},{8,6},{9,7},{10,8},{11,9},{12,... | collective-permute-start | bytes 786440 | tf_op jit(solution)/shard_map/ppermute | solution.py:18
  82.0 10.6 %collective-permute-start.2 = (bf16[4,128,256]{2,1,0:T(8,128)(2,1)S(1)}, bf16[4,128,256]{2,1,0:T(8,128)(2,1)S(1)}, u32[]{:S(2)}, u32[]{:S(2)}) collective-permute-start(bf16[4,128,256]{2,1,0:T(8,128)(2,1)S(1)} %get-tuple-element.30), channel_id=1, source_target_pairs={{62,0},{63,1},{0,2},{1,3},{2,4},{3,5},{4,6},{5,7},{6,8},{7,9},{8,1... | collective-permute-start | bytes 786440 | tf_op jit(solution)/shard_map/ppermute | solution.py:18
  92.8 1.1 copy-start.2
  104.5 9.2 %collective-permute-start.6 = (bf16[4,128,256]{2,1,0:T(8,128)(2,1)S(1)}, bf16[4,128,256]{2,1,0:T(8,128)(2,1)S(1)}, u32[]{:S(2)}, u32[]{:S(2)}) collective-permute-start(bf16[4,128,256]{2,1,0:T(8,128)(2,1)S(1)} %get-tuple-element.26), channel_id=1, source_target_pairs={{63,0},{0,1},{1,2},{2,3},{3,4},{4,5},{5,6},{6,7},{7,8},{8,9},{9,10... | collective-permute-start | bytes 786440 | tf_op jit(solution)/shard_map/ppermute | solution.py:18
  104.6 10.3 %collective-permute-start.7 = (bf16[4,128,256]{2,1,0:T(8,128)(2,1)S(1)}, bf16[4,128,256]{2,1,0:T(8,128)(2,1)S(1)}, u32[]{:S(2)}, u32[]{:S(2)}) collective-permute-start(bf16[4,128,256]{2,1,0:T(8,128)(2,1)S(1)} %get-tuple-element.25), channel_id=1, source_target_pairs={{1,0},{2,1},{3,2},{4,3},{5,4},{6,5},{7,6},{8,7},{9,8},{10,9},{11,1... | collective-permute-start | bytes 786440 | tf_op jit(solution)/shard_map/ppermute | solution.py:18
  109.7 14.4 %collective-permute-start.11 = (bf16[4,128,256]{2,1,0:T(8,128)(2,1)S(1)}, bf16[4,128,256]{2,1,0:T(8,128)(2,1)S(1)}, u32[]{:S(2)}, u32[]{:S(2)}) collective-permute-start(bf16[4,128,256]{2,1,0:T(8,128)(2,1)S(1)} %get-tuple-element.21), channel_id=1, source_target_pairs={{64,0},{128,64},{192,128},{0,192},{65,1},{129,65},{193,129},{1,193... | collective-permute-start | bytes 786440 | tf_op jit(solution)/shard_map/ppermute | solution.py:18
  109.8 14.3 %collective-permute-start.10 = (bf16[4,128,256]{2,1,0:T(8,128)(2,1)S(1)}, bf16[4,128,256]{2,1,0:T(8,128)(2,1)S(1)}, u32[]{:S(2)}, u32[]{:S(2)}) collective-permute-start(bf16[4,128,256]{2,1,0:T(8,128)(2,1)S(1)} %get-tuple-element.22), channel_id=1, source_target_pairs={{192,0},{0,64},{64,128},{128,192},{193,1},{1,65},{65,129},{129,193... | collective-permute-start | bytes 786440 | tf_op jit(solution)/shard_map/ppermute | solution.py:18
  112.9 11.1 %collective-permute-start.9 = (bf16[4,128,256]{2,1,0:T(8,128)(2,1)S(1)}, bf16[4,128,256]{2,1,0:T(8,128)(2,1)S(1)}, u32[]{:S(2)}, u32[]{:S(2)}) collective-permute-start(bf16[4,128,256]{2,1,0:T(8,128)(2,1)S(1)} %get-tuple-element.23), channel_id=1, source_target_pairs={{2,0},{3,1},{4,2},{5,3},{6,4},{7,5},{8,6},{9,7},{10,8},{11,9},{12,... | collective-permute-start | bytes 786440 | tf_op jit(solution)/shard_map/ppermute | solution.py:18
  113.7 10.3 %collective-permute-start.8 = (bf16[4,128,256]{2,1,0:T(8,128)(2,1)S(1)}, bf16[4,128,256]{2,1,0:T(8,128)(2,1)S(1)}, u32[]{:S(2)}, u32[]{:S(2)}) collective-permute-start(bf16[4,128,256]{2,1,0:T(8,128)(2,1)S(1)} %get-tuple-element.24), channel_id=1, source_target_pairs={{62,0},{63,1},{0,2},{1,3},{2,4},{3,5},{4,6},{5,7},{6,8},{7,9},{8,1... | collective-permute-start | bytes 786440 | tf_op jit(solution)/shard_map/ppermute | solution.py:18
  124.0 3.3 %copy-start.1 = (bf16[1,1,1536,256]{3,2,1,0:T(8,128)(2,1)S(1)}, bf16[1,1,1536,256]{3,2,1,0:T(8,128)(2,1)}, u32[]{:S(2)}) copy-start(bf16[1,1,1536,256]{3,2,1,0:T(8,128)(2,1)} %param.13) | copy-start | bytes 2359300
  176.9 9.2 %collective-permute-start.12 = (bf16[4,128,256]{2,1,0:T(8,128)(2,1)S(1)}, bf16[4,128,256]{2,1,0:T(8,128)(2,1)S(1)}, u32[]{:S(2)}, u32[]{:S(2)}) collective-permute-start(bf16[4,128,256]{2,1,0:T(8,128)(2,1)S(1)} %get-tuple-element.20), channel_id=1, source_target_pairs={{63,0},{0,1},{1,2},{2,3},{3,4},{4,5},{5,6},{6,7},{7,8},{8,9},{9,10... | collective-permute-start | bytes 786440 | tf_op jit(solution)/shard_map/ppermute | solution.py:18
  177.1 10.9 %collective-permute-start.13 = (bf16[4,128,256]{2,1,0:T(8,128)(2,1)S(1)}, bf16[4,128,256]{2,1,0:T(8,128)(2,1)S(1)}, u32[]{:S(2)}, u32[]{:S(2)}) collective-permute-start(bf16[4,128,256]{2,1,0:T(8,128)(2,1)S(1)} %get-tuple-element.19), channel_id=1, source_target_pairs={{1,0},{2,1},{3,2},{4,3},{5,4},{6,5},{7,6},{8,7},{9,8},{10,9},{11,1... | collective-permute-start | bytes 786440 | tf_op jit(solution)/shard_map/ppermute | solution.py:18
  182.1 16.5 %collective-permute-start.17 = (bf16[4,128,256]{2,1,0:T(8,128)(2,1)S(1)}, bf16[4,128,256]{2,1,0:T(8,128)(2,1)S(1)}, u32[]{:S(2)}, u32[]{:S(2)}) collective-permute-start(bf16[4,128,256]{2,1,0:T(8,128)(2,1)S(1)} %get-tuple-element.15), channel_id=1, source_target_pairs={{64,0},{128,64},{192,128},{0,192},{65,1},{129,65},{193,129},{1,193... | collective-permute-start | bytes 786440 | tf_op jit(solution)/shard_map/ppermute | solution.py:18
  182.1 15.8 %collective-permute-start.16 = (bf16[4,128,256]{2,1,0:T(8,128)(2,1)S(1)}, bf16[4,128,256]{2,1,0:T(8,128)(2,1)S(1)}, u32[]{:S(2)}, u32[]{:S(2)}) collective-permute-start(bf16[4,128,256]{2,1,0:T(8,128)(2,1)S(1)} %get-tuple-element.16), channel_id=1, source_target_pairs={{192,0},{0,64},{64,128},{128,192},{193,1},{1,65},{65,129},{129,193... | collective-permute-start | bytes 786440 | tf_op jit(solution)/shard_map/ppermute | solution.py:18
  185.3 11.8 %collective-permute-start.15 = (bf16[4,128,256]{2,1,0:T(8,128)(2,1)S(1)}, bf16[4,128,256]{2,1,0:T(8,128)(2,1)S(1)}, u32[]{:S(2)}, u32[]{:S(2)}) collective-permute-start(bf16[4,128,256]{2,1,0:T(8,128)(2,1)S(1)} %get-tuple-element.17), channel_id=1, source_target_pairs={{2,0},{3,1},{4,2},{5,3},{6,4},{7,5},{8,6},{9,7},{10,8},{11,9},{12,... | collective-permute-start | bytes 786440 | tf_op jit(solution)/shard_map/ppermute | solution.py:18
  186.1 10.3 %collective-permute-start.14 = (bf16[4,128,256]{2,1,0:T(8,128)(2,1)S(1)}, bf16[4,128,256]{2,1,0:T(8,128)(2,1)S(1)}, u32[]{:S(2)}, u32[]{:S(2)}) collective-permute-start(bf16[4,128,256]{2,1,0:T(8,128)(2,1)S(1)} %get-tuple-element.18), channel_id=1, source_target_pairs={{62,0},{63,1},{0,2},{1,3},{2,4},{3,5},{4,6},{5,7},{6,8},{7,9},{8,1... | collective-permute-start | bytes 786440 | tf_op jit(solution)/shard_map/ppermute | solution.py:18
  216.6 9.2 %collective-permute-start.18 = (bf16[4,128,256]{2,1,0:T(8,128)(2,1)S(1)}, bf16[4,128,256]{2,1,0:T(8,128)(2,1)S(1)}, u32[]{:S(2)}, u32[]{:S(2)}) collective-permute-start(bf16[4,128,256]{2,1,0:T(8,128)(2,1)S(1)} %get-tuple-element.14), channel_id=1, source_target_pairs={{63,0},{0,1},{1,2},{2,3},{3,4},{4,5},{5,6},{6,7},{7,8},{8,9},{9,10... | collective-permute-start | bytes 786440 | tf_op jit(solution)/shard_map/ppermute | solution.py:18
  216.7 11.0 %collective-permute-start.19 = (bf16[4,128,256]{2,1,0:T(8,128)(2,1)S(1)}, bf16[4,128,256]{2,1,0:T(8,128)(2,1)S(1)}, u32[]{:S(2)}, u32[]{:S(2)}) collective-permute-start(bf16[4,128,256]{2,1,0:T(8,128)(2,1)S(1)} %get-tuple-element.13), channel_id=1, source_target_pairs={{1,0},{2,1},{3,2},{4,3},{5,4},{6,5},{7,6},{8,7},{9,8},{10,9},{11,1... | collective-permute-start | bytes 786440 | tf_op jit(solution)/shard_map/ppermute | solution.py:18
  221.8 16.5 %collective-permute-start.23 = (bf16[4,128,256]{2,1,0:T(8,128)(2,1)S(1)}, bf16[4,128,256]{2,1,0:T(8,128)(2,1)S(1)}, u32[]{:S(2)}, u32[]{:S(2)}) collective-permute-start(bf16[4,128,256]{2,1,0:T(8,128)(2,1)S(1)} %get-tuple-element.9), channel_id=1, source_target_pairs={{64,0},{128,64},{192,128},{0,192},{65,1},{129,65},{193,129},{1,193... | collective-permute-start | bytes 786440 | tf_op jit(solution)/shard_map/ppermute | solution.py:18
  221.8 15.8 %collective-permute-start.22 = (bf16[4,128,256]{2,1,0:T(8,128)(2,1)S(1)}, bf16[4,128,256]{2,1,0:T(8,128)(2,1)S(1)}, u32[]{:S(2)}, u32[]{:S(2)}) collective-permute-start(bf16[4,128,256]{2,1,0:T(8,128)(2,1)S(1)} %get-tuple-element.10), channel_id=1, source_target_pairs={{192,0},{0,64},{64,128},{128,192},{193,1},{1,65},{65,129},{129,193... | collective-permute-start | bytes 786440 | tf_op jit(solution)/shard_map/ppermute | solution.py:18
  225.0 11.8 %collective-permute-start.21 = (bf16[4,128,256]{2,1,0:T(8,128)(2,1)S(1)}, bf16[4,128,256]{2,1,0:T(8,128)(2,1)S(1)}, u32[]{:S(2)}, u32[]{:S(2)}) collective-permute-start(bf16[4,128,256]{2,1,0:T(8,128)(2,1)S(1)} %get-tuple-element.11), channel_id=1, source_target_pairs={{2,0},{3,1},{4,2},{5,3},{6,4},{7,5},{8,6},{9,7},{10,8},{11,9},{12,... | collective-permute-start | bytes 786440 | tf_op jit(solution)/shard_map/ppermute | solution.py:18
  225.8 10.3 %collective-permute-start.20 = (bf16[4,128,256]{2,1,0:T(8,128)(2,1)S(1)}, bf16[4,128,256]{2,1,0:T(8,128)(2,1)S(1)}, u32[]{:S(2)}, u32[]{:S(2)}) collective-permute-start(bf16[4,128,256]{2,1,0:T(8,128)(2,1)S(1)} %get-tuple-element.12), channel_id=1, source_target_pairs={{62,0},{63,1},{0,2},{1,3},{2,4},{3,5},{4,6},{5,7},{6,8},{7,9},{8,1... | collective-permute-start | bytes 786440 | tf_op jit(solution)/shard_map/ppermute | solution.py:18
  (3 other events, 2.7 us)
where the time goes:
time: 250 us; the launch traced here: 245 us
  waiting for transfers between devices  68.4 us (27%)
  starting transfers between devices  61.1 us (24%)
  local copies, waits for them, and re-layouts  46.4 us (19%)
  blocking collectives  32.3 us (13%)
  matrix products  19.2 us (8%)
  other arithmetic  17 us (7%)
    ppermute x24, starting transfers between devices, passed_along(): return lax.ppermute(block, axis, route)  38.3 us
    ppermute x24, waiting for transfers between devices, passed_along(): return lax.ppermute(block, axis, route)  36.6 us
    all_to_all x1, blocking collectives, from_everyone(): lax.all_to_all(jnp.broadcast_to(x[None], (peers, *x.shape)), axis, 0, 0,...  32.3 us
    all_to_all x2, waiting for transfers between devices, from_everyone(): lax.all_to_all(jnp.broadcast_to(x[None], (peers, *x.shape)), axis, 0, 0,...  18.9 us
    all_to_all x2, starting transfers between devices, from_everyone(): lax.all_to_all(jnp.broadcast_to(x[None], (peers, *x.shape)), axis, 0, 0,...  17.1 us
    all_to_all x1, waiting for transfers between devices, on_device(): lax.all_to_all(wanted_columns.astype(jnp.bfloat16), 'sub', split_axis=1,...  12.9 us
    unnamed x37, local copies, waits for them, and re-layouts  10.6 us
    gather x4, local copies, waits for them, and re-layouts, jump(): remote = jnp.take(received, read_codes, axis=0)  9.94 us
  transfers between devices with their start and end apart: 27, of which 11 were waited for; matrix products, arithmetic and copies ran while one was open for 6% of the time, Pallas kernels for 0%

commit v1 on v0

v1 whole, which is shorter than its diff:
```python
import functools

import jax
import jax.numpy as jnp
from jax import lax
from jax.experimental import pallas as pl
from jax.experimental.pallas import tpu as pltpu
from jax.sharding import PartitionSpec as P

BLK = 128
DIRS = 6
CAP = 4
ITERS = 2
SLOTS = DIRS * CAP
PAD = 16
CH = 2
CORES = 2
TILE = 256
OFFSETS = (1, -1, 2, -2)
ORDER = (2, 3, 0, 1, 4, 5)
MESH = pl.DeviceIdType.MESH
BF = jnp.bfloat16
F32 = jnp.float32


def kernel(
    zs, ys, gs,
    load_hbm, a_hbm, s_hbm, basis_ref, cinv_ref, map_ref, mult_ref, code_ref, send_ref,
    out_hbm,
    load_v, a_v, s_v, load_sem, a_sem, s_sem, out_sem,
    bcol, brcol, brow, bslab, brecv, bs_sem, br_sem,
    mown, mrow, mtile, mall, ms_sem, mr_sem, zs_sem, zr_sem,
    onehot, selbuf, colz, colall, cs_sem, cr_sem, ys_sem, yr_sem, wbuf,
    x, slab, rv0, rv1, rv2, rv3, rv4, rv5, rv6, rv7, es_sem, er_sem,
    sc, mul, res,
    pf, psend, prow, pall, ps_sem, pr_sem, qs_sem, qr_sem,
    crow, cout, cin, cloc, ks_sem, kr_sem, cslab, cv0, cv1, cv2, cv3, ts_sem, tr_sem,
):
    nb, cases = load_v.shape
    nblk = nb // BLK
    cw = cases // CH
    rows = zs * ys * CORES
    rowdev = ys * CORES
    recv = (rv0, rv1, rv2, rv3, rv4, rv5, rv6, rv7)
    crecv = (cv0, cv1, cv2, cv3)
    g = lax.axis_index("group")
    s = lax.axis_index("sub")
    c = lax.rem(s, CORES)
    zy = lax.div(s, CORES)
    y = lax.rem(zy, ys)
    z = lax.div(zy, ys)
    yc = y * CORES + c

    def sub_at(zz, yy, cc):
        return (zz * ys + yy) * CORES + cc

    def row_peer(dy, dc):
        yy = lax.rem(y + dy, ys)
        cc = lax.rem(c + dc, CORES)
        return (g, sub_at(z, yy, cc))

    def col_peer(dz):
        return (g, sub_at(lax.rem(z + dz, zs), y, c))

    def reader(d):
        if d < 4:
            return (g, lax.rem(s + OFFSETS[d] + rows, rows))
        return (lax.rem(g + (1 if d == 4 else gs - 1), gs), s)

    row_steps = [(dy, dc) for dy in range(ys) for dc in range(CORES) if (dy, dc) != (0, 0)]
    col_steps = list(range(1, zs))
    started = []

    def remote(src, dst, ssem, rsem, dev):
        return pltpu.make_async_remote_copy(
            src_ref=src, dst_ref=dst, send_sem=ssem, recv_sem=rsem,
            device_id=dev, device_id_type=MESH,
        )

    barrier = pltpu.get_barrier_semaphore()
    peers = [row_peer(dy, dc) for dy, dc in row_steps]
    peers += [col_peer(dz) for dz in col_steps]
    peers += [reader(d) for d in range(DIRS)]
    for peer in peers:
        pl.semaphore_signal(barrier, inc=1, device_id=peer, device_id_type=MESH)
    load_copy = pltpu.make_async_copy(load_hbm.at[0, 0], load_v, load_sem)
    load_copy.start()
    tiles = nb // TILE

    def a_copy(t):
        part = pl.ds(t * TILE, TILE)
        return pltpu.make_async_copy(a_hbm.at[0, 0, part], a_v.at[part], a_sem.at[t])

    for t in range(tiles):
        a_copy(t).start()
    s_copy = pltpu.make_async_copy(s_hbm.at[0, 0], s_v, s_sem)
    s_copy.start()

    lane = lax.broadcasted_iota(jnp.int32, (8, 128), 1)
    mine = jnp.full((8, 128), -1, jnp.int32)
    for b in range(nblk):
        line = basis_ref[:, b * BLK:(b + 1) * BLK]
        brow[b:b + 1, :] = line
        bcol[b] = jnp.transpose(jnp.broadcast_to(line, (BLK, BLK)))
        mine = jnp.where(lane == b, map_ref[0, b], mine)
    mown[...] = mine
    bslab[...] = jnp.zeros_like(bslab)
    for k in range(SLOTS):
        at = (k // CAP) * 8 + k % CAP
        bslab[at:at + 1, :] = brow[pl.ds(jnp.maximum(send_ref[0, k], 0), 1), :]
    pl.semaphore_wait(barrier, len(peers))

    map_row = []
    for n, (dy, dc) in enumerate(row_steps):
        map_row.append(remote(mown, mrow.at[yc], ms_sem.at[n], mr_sem.at[n], row_peer(dy, dc)))
        map_row[-1].start()
    basis_out = []
    for d in range(DIRS):
        part = pl.ds(d * 8, 8)
        basis_out.append(remote(bslab.at[part], brecv.at[part], bs_sem.at[d], br_sem.at[d], reader(d)))
        basis_out[-1].start()
    started += map_row + basis_out
    mrow[yc] = mine

    def slab_copy(e, h, d):
        part = pl.ds(d * CAP, CAP)
        n = (e * CH + h) * DIRS + d
        return remote(
            slab.at[e * CH + h, part], recv[e * CH + h].at[part],
            es_sem.at[n], er_sem.at[n], reader(d),
        )

    def pack(e, h):
        for d in ORDER:
            for j in range(CAP):
                k = d * CAP + j
                slab[e * CH + h, k] = x[h, jnp.maximum(send_ref[0, k], 0)]
            copy = slab_copy(e, h, d)
            copy.start()
            started.append(copy)

    def wait_slabs(e, h):
        for d in ORDER:
            slab_copy(e, h, d).wait_recv()

    def p_send(i, h):
        psend[i, h] = pf[h].astype(BF)
        dc = lax.rem(c + h, CORES)
        for dy in range(ys):
            n = (i * CH + h) * ys + dy
            copy = remote(
                psend.at[i, h], prow.at[i, yc], ps_sem.at[n],
                pr_sem.at[i * rowdev + dy * CORES + dc], row_peer(dy, dc),
            )
            if dy == 0:
                @pl.when(dc != 0)
                def _():
                    copy.start()

                @pl.when(dc == 0)
                def _():
                    prow[i, yc] = pf[h].astype(BF)
            else:
                copy.start()

    def p_wait_sends():
        for i in range(ITERS):
            for h in range(CH):
                dc = lax.rem(c + h, CORES)
                for dy in range(ys):
                    n = (i * CH + h) * ys + dy
                    copy = remote(
                        psend.at[i, h], prow.at[i, yc], ps_sem.at[n],
                        pr_sem.at[i * rowdev + dy * CORES + dc], row_peer(dy, dc),
                    )
                    if dy == 0:
                        @pl.when(dc != 0)
                        def _():
                            copy.wait_send()
                    else:
                        copy.wait_send()

    def q_copy(i, n, dz):
        return remote(
            prow.at[i], pall.at[i, z], qs_sem.at[i * zs + n], qr_sem.at[i * zs + n], col_peer(dz)
        )

    def relay(i):
        for dy, dc in row_steps:
            remote(
                psend.at[i, 0], prow.at[i, 0], ps_sem.at[0],
                pr_sem.at[i * rowdev + dy * CORES + dc], row_peer(dy, dc),
            ).wait_recv()
        for n, dz in enumerate(col_steps):
            q_copy(i, n, dz).start()
        pall[i, z] = prow[i]

    def partner_copy(i):
        return remote(cout.at[i], cin.at[i], ks_sem.at[i], kr_sem.at[i], row_peer(0, 1))

    def coarse(i):
        for n, dz in enumerate(col_steps):
            q_copy(i, n, dz).wait_recv()
        every = pall[i].reshape(rows * PAD, cw)
        crow[...] = jnp.dot(wbuf[...], every, preferred_element_type=F32).reshape(rowdev, PAD, cw)
        cout[i] = crow[y * CORES + (1 - c)]
        partner_copy(i).start()

    def t_copy(i, h, d):
        part = pl.ds(d * 8, 8)
        n = (i * CH + h) * DIRS + d
        return remote(
            cslab.at[i * CH + h, part], crecv[i * CH + h].at[part],
            ts_sem.at[n], tr_sem.at[n], reader(d),
        )

    def spread(i, h):
        @pl.when(c == h)
        def _():
            cloc[h] = crow[yc]

        @pl.when(c != h)
        def _():
            partner_copy(i).wait_recv()
            cloc[h] = cin[i]

        cslab[i * CH + h] = jnp.zeros(cslab.shape[1:], F32)
        for d in range(DIRS):
            for j in range(CAP):
                k = d * CAP + j
                at = d * 8 + j
                cslab[i * CH + h, at:at + 1, :] = cloc[h, pl.ds(jnp.maximum(send_ref[0, k], 0), 1), :]
            copy = t_copy(i, h, d)
            copy.start()
            started.append(copy)

    def code_row(b):
        code = code_ref[0, b]
        return code, (code // CAP) * 8 + code % CAP

    def weight(b):
        return 1.0 / jnp.full((1, 128), mult_ref[0, b].astype(F32))

    def keep(b, h, disp):
        pf[h, pl.ds(b, 1), :] = jnp.sum(bcol[b] * disp, axis=0, keepdims=True)
        x[h, b] = disp.astype(BF)

    per = TILE // BLK

    def first_solve():
        load_copy.wait()

        def step(t, carry):
            a_copy(t).wait()
            acc = jnp.dot(a_v[pl.ds(t * TILE, TILE), :], load_v[...], preferred_element_type=F32)
            for i in range(per):
                for h in range(CH):
                    keep(t * per + i, h, acc[i * BLK:(i + 1) * BLK, h * cw:(h + 1) * cw])
            return carry

        lax.fori_loop(0, tiles, step, 0)

    def solve(h):
        def step(t, carry):
            acc = jnp.dot(a_v[pl.ds(t * TILE, TILE), :], res[h], preferred_element_type=F32)
            for i in range(per):
                keep(t * per + i, h, acc[i * BLK:(i + 1) * BLK])
            return carry

        lax.fori_loop(0, tiles, step, 0)

    def scale(i, h):
        e = 2 * i
        wait_slabs(e, h)
        for d in range(DIRS):
            t_copy(i, h, d).wait_recv()

        def step(b, carry):
            code, at = code_row(b)
            own = x[h, b].astype(F32) + bcol[b] * cloc[h, pl.ds(b, 1), :]
            far = recv[e * CH + h][code].astype(F32) + brcol[b] * crecv[i * CH + h][pl.ds(at, 1), :]
            sc[h, pl.ds(b * BLK, BLK), :] = ((own - far) * weight(b)).astype(BF)
            return carry

        lax.fori_loop(0, nblk, step, 0)

    def dirichlet(h):
        def step(t, carry):
            acc = jnp.dot(s_v[pl.ds(t * TILE, TILE), :], sc[h], preferred_element_type=F32)
            for i in range(per):
                b = t * per + i
                x[h, b] = (acc[i * BLK:(i + 1) * BLK] * weight(b)).astype(BF)
            return carry

        lax.fori_loop(0, tiles, step, 0)

    def update(i, h):
        e = 2 * i + 1
        wait_slabs(e, h)
        cols = slice(h * cw, (h + 1) * cw)

        def step(b, carry):
            part = pl.ds(b * BLK, BLK)
            new = x[h, b].astype(F32) - recv[e * CH + h][code_ref[0, b]].astype(F32)
            if i == 0:
                res[h, part, :] = (load_v[part, cols].astype(F32) - new).astype(BF)
            else:
                new = mul[part, cols] + new
            mul[part, cols] = new
            return carry

        lax.fori_loop(0, nblk, step, 0)

    def column_maps():
        for n in range(len(row_steps)):
            map_row[n].wait_recv()
        line = lax.broadcasted_iota(jnp.int32, (8, 128), 0)
        tile = jnp.full((8, 128), -1, jnp.int32)
        for n in range(rowdev):
            tile = jnp.where(line == n, mrow[n], tile)
        mtile[...] = tile
        copies = []
        for n, dz in enumerate(col_steps):
            copies.append(remote(mtile, mall.at[z], zs_sem.at[n], zr_sem.at[n], col_peer(dz)))
            copies[-1].start()
        mall[z] = tile
        started.extend(copies)
        return copies

    def columns(copies):
        for copy in copies:
            copy.wait_recv()
        grid = jnp.transpose(mall[...].reshape(zs * 8, 128).astype(F32))
        order = rows * PAD
        width = onehot.shape[1]
        ids = lax.broadcasted_iota(jnp.int32, (PAD, width), 1).astype(F32)
        for zz in range(zs):
            for r in range(rowdev):
                at = (zz * rowdev + r) * PAD
                n = zz * 8 + r
                hit = jnp.broadcast_to(grid[:PAD, n:n + 1], (PAD, width)) == ids
                onehot[at:at + PAD, :] = jnp.where(hit, 1.0, 0.0).astype(BF)
        picked = lax.dot_general(
            cinv_ref[0].astype(BF), onehot[...], (((1,), (1,)), ((), ())), preferred_element_type=F32
        ).astype(BF)
        lanes = rowdev * PAD
        copies = []
        for zz in range(zs):
            selbuf[zz] = picked[:, zz * lanes:(zz + 1) * lanes]
        for n, dz in enumerate(col_steps):
            zz = lax.rem(z + dz, zs)
            copies.append(remote(selbuf.at[zz], colz.at[z], cs_sem.at[n], cr_sem.at[n], col_peer(dz)))
            copies[-1].start()
        colz[z] = selbuf[z]
        started.extend(copies)
        return copies

    def share_columns(copies):
        for copy in copies:
            copy.wait_recv()
        out = []
        for n, (dy, dc) in enumerate(row_steps):
            out.append(remote(colz, colall.at[:, yc], ys_sem.at[n], yr_sem.at[n], row_peer(dy, dc)))
            out[-1].start()
        colall[:, yc] = colz[...]
        started.extend(out)
        return out

    def coarse_rows(copies):
        for copy in copies:
            copy.wait_recv()
        mat = colall[...].reshape(onehot.shape[1], rowdev * PAD)
        wide = jnp.dot(onehot[...], mat, preferred_element_type=F32)
        wbuf[...] = jnp.transpose(wide).astype(BF)

    pf[...] = jnp.zeros_like(pf)
    first_solve()
    for h in range(CH):
        p_send(0, h)
    for h in range(CH):
        pack(0, h)
    map_col = column_maps()
    relay(0)
    for copy in basis_out:
        copy.wait_recv()
    for b in range(nblk):
        _, at = code_row(b)
        brcol[b] = jnp.transpose(jnp.broadcast_to(brecv[pl.ds(at, 1), :], (BLK, BLK)))
    col_out = columns(map_col)
    row_out = share_columns(col_out)
    coarse_rows(row_out)
    coarse(0)
    for h in range(CH):
        spread(0, h)
    s_copy.wait()
    for h in range(CH):
        scale(0, h)
        dirichlet(h)
        pack(1, h)
    for h in range(CH):
        update(0, h)
        solve(h)
        p_send(1, h)
        pack(2, h)

        @pl.when(c == h)
        def _():
            relay(1)

    for h in range(CH):
        @pl.when(c == h)
        def _():
            coarse(1)

        spread(1, h)
        scale(1, h)
        dirichlet(h)
        pack(3, h)
    outs = []
    for h in range(CH):
        update(1, h)
        cols = pl.ds(h * cw, cw)
        outs.append(pltpu.make_async_copy(mul.at[:, cols], out_hbm.at[0, 0, :, cols], out_sem.at[h]))
        outs[-1].start()

    for copy in started:
        copy.wait_send()
    p_wait_sends()
    for i in range(ITERS):
        for n, dz in enumerate(col_steps):
            q_copy(i, n, dz).wait_send()
        partner_copy(i).wait_send()
    for copy in outs:
        copy.wait()


def on_device(zs, ys, gs, *args):
    (load_cases, inv_schur, schur_blocks, coarse_basis, coarse_map,
     multiplicity, recv_code, send_blocks, coarse_inv) = args
    _, _, nb, cases = load_cases.shape
    nblk = nb // BLK
    cw = cases // CH
    own, nc = coarse_inv.shape[1:]
    rowdev = ys * CORES
    rows = zs * rowdev
    tiles = nb // TILE
    dma = pltpu.SemaphoreType.DMA
    vm = pltpu.VMEM
    exchanges = 2 * ITERS * CH
    scratch = [
        vm((nb, cases), BF), vm((nb, nb), BF), vm((nb, nb), BF),
        dma, dma((tiles,)), dma, dma((CH,)),
        vm((nblk, BLK, BLK), F32), vm((nblk, BLK, BLK), F32), vm((PAD, BLK), F32),
        vm((DIRS * 8, BLK), F32), vm((DIRS * 8, BLK), F32), dma((DIRS,)), dma((DIRS,)),
        vm((8, 128), jnp.int32), vm((rowdev, 8, 128), jnp.int32), vm((8, 128), jnp.int32),
        vm((zs, 8, 128), jnp.int32), dma((rowdev,)), dma((rowdev,)), dma((zs,)), dma((zs,)),
        vm((rows * PAD, nc), BF), vm((zs, own, rowdev * PAD), BF), vm((zs, own, rowdev * PAD), BF),
        vm((zs, rowdev, own, rowdev * PAD), BF),
        dma((zs,)), dma((zs,)), dma((rowdev,)), dma((rowdev,)), vm((rowdev * PAD, rows * PAD), BF),
        vm((CH, nblk, BLK, cw), BF), vm((exchanges, SLOTS, BLK, cw), BF),
        *[vm((SLOTS, BLK, cw), BF) for _ in range(exchanges)],
        dma((exchanges * DIRS,)), dma((exchanges * DIRS,)),
        vm((CH, nb, cw), BF), vm((nb, cases), F32), vm((CH, nb, cw), BF),
        vm((CH, PAD, cw), F32), vm((ITERS, CH, PAD, cw), BF), vm((ITERS, rowdev, PAD, cw), BF),
        vm((ITERS, zs, rowdev, PAD, cw), BF),
        dma((ITERS * CH * ys,)), dma((ITERS * rowdev,)), dma((ITERS * zs,)), dma((ITERS * zs,)),
        vm((rowdev, PAD, cw), F32), vm((ITERS, PAD, cw), F32), vm((ITERS, PAD, cw), F32),
        vm((CH, PAD, cw), F32), dma((ITERS,)), dma((ITERS,)),
        vm((ITERS * CH, DIRS * 8, cw), F32),
        *[vm((DIRS * 8, cw), F32) for _ in range(ITERS * CH)],
        dma((ITERS * CH * DIRS,)), dma((ITERS * CH * DIRS,)),
    ]
    hbm = pl.BlockSpec(memory_space=pl.ANY)
    inside = pl.BlockSpec(memory_space=pltpu.VMEM)
    scalars = pl.BlockSpec(memory_space=pltpu.SMEM)
    return pl.pallas_call(
        functools.partial(kernel, zs, ys, gs),
        out_shape=jax.ShapeDtypeStruct(load_cases.shape, F32),
        in_specs=[hbm, hbm, hbm, inside, inside, scalars, scalars, scalars, scalars],
        out_specs=hbm,
        scratch_shapes=scratch,
        compiler_params=pltpu.CompilerParams(
            collective_id=0, has_side_effects=True, vmem_limit_bytes=60 * 1024 * 1024
        ),
        name="feti",
    )(
        load_cases, inv_schur, schur_blocks, coarse_basis[0], coarse_inv,
        coarse_map[0], multiplicity[0], recv_code[0], send_blocks[0],
    )


def build(mesh, zs, ys):
    wide = P("group", "sub", None, None)
    thin = P("group", "sub", None)
    return jax.shard_map(
        functools.partial(on_device, zs, ys, mesh.shape["group"]),
        mesh=mesh,
        in_specs=(wide, wide, wide, thin, thin, thin, thin, thin, thin),
        out_specs=wide,
        check_vma=False,
    )


def solution(mesh):
    ys = 4
    return build(mesh, mesh.shape["sub"] // (ys * CORES), ys)
```

time: 250 us -> 98.3 us (0.39)
  the two profiles are of different devices: /device:TPU:6 before, /device:TPU:1 now
where the time goes in v1:
time: 98.3 us; the launch traced here: 97.1 us
  Pallas kernels  94.4 us (96%)
  local copies, waits for them, and re-layouts  2.65 us (3%)
    pallas_call x1, Pallas kernels, on_device(): pl.pallas_call(functools.partial(kernel, zs, ys, gs), out_shape=jax.Shape...  94.4 us
    unnamed x1, local copies, waits for them, and re-layouts  2.65 us

profile of v1, /device:TPU:1, one launch (start us, length us, event | category | flops | bytes accessed | tf_op | source)
XLA Modules:
  0.0 97.1 jit_solution(3619754150732587877)
XLA Ops:
  0.0 94.4 %feti.1 = f32[1,1,1536,256]{3,2,1,0:T(8,128)} custom-call(bf16[1,1,1536,256]{3,2,1,0:T(8,128)(2,1)} %load_hbm.1, bf16[1,1,1536,1536]{3,2,1,0:T(8,128)(2,1)} %a_hbm.1, bf16[1,1,1536,1536]{3,2,1,0:T(8,128)(2,1)} %s_hbm.1, f32[1,1536]{1,0:T(1,128)} %bitcast.5, f32[1,16,1024]{2,1,0:T(8,128)} %cinv_ref.1, s32[1,12]{1,0:T(1,128)} %bitcast.6, s32[1,12]{1,0:T(1,128)} %bitcast.7, ...), custom_call_target="tpu_custom_call" | custom-call | tf_op jit(solution)/shard_map/feti/pallas_call | solution.py:476
  94.4 2.7 %copy.11 = f32[1,1,1536,256]{3,2,1,0:T(8,128)} copy(f32[1,1,1536,256]{3,2,1,0:T(8,128)} %feti.1) | data formatting | bytes 3145728

commit v2 on v1

--- a/solution.py
+++ b/solution.py
@@ -17,7 +17,9 @@
 CORES = 2
 TILE = 256
 OFFSETS = (1, -1, 2, -2)
-ORDER = (2, 3, 0, 1, 4, 5)
+ALONG = (2, 3, 0, 1)
+ACROSS = (4, 5)
+ORDER = ALONG + ACROSS
 MESH = pl.DeviceIdType.MESH
 BF = jnp.bfloat16
 F32 = jnp.float32
@@ -25,16 +27,17 @@
 
 def kernel(
     zs, ys, gs,
-    load_hbm, a_hbm, s_hbm, basis_ref, cinv_ref, map_ref, mult_ref, code_ref, send_ref,
+    load_hbm, a_hbm, s_hbm, basis_hbm, cinv_hbm, map_hbm, mult_hbm, code_hbm, send_hbm,
     out_hbm,
+    basis_ref, cinv_ref, map_ref, mult_ref, code_ref, send_ref, small_sem,
     load_v, a_v, s_v, load_sem, a_sem, s_sem, out_sem,
     bcol, brcol, brow, bslab, brecv, bs_sem, br_sem,
     mown, mrow, mtile, mall, ms_sem, mr_sem, zs_sem, zr_sem,
-    onehot, selbuf, colz, colall, cs_sem, cr_sem, ys_sem, yr_sem, wbuf,
+    onehot, twohot, selbuf, colz, colt, colall, cs_sem, cr_sem, ys_sem, yr_sem, wbuf,
     x, slab, rv0, rv1, rv2, rv3, rv4, rv5, rv6, rv7, es_sem, er_sem,
     sc, mul, res,
     pf, psend, prow, pall, ps_sem, pr_sem, qs_sem, qr_sem,
-    crow, cout, cin, cloc, ks_sem, kr_sem, cslab, cv0, cv1, cv2, cv3, ts_sem, tr_sem,
+    cres, cin, cloc, cfar, cnear, ks_sem, kr_sem, ts_sem, tr_sem,
 ):
     nb, cases = load_v.shape
     nblk = nb // BLK
@@ -42,7 +45,6 @@
     rows = zs * ys * CORES
     rowdev = ys * CORES
     recv = (rv0, rv1, rv2, rv3, rv4, rv5, rv6, rv7)
-    crecv = (cv0, cv1, cv2, cv3)
     g = lax.axis_index("group")
     s = lax.axis_index("sub")
     c = lax.rem(s, CORES)
@@ -62,10 +64,11 @@
     def col_peer(dz):
         return (g, sub_at(lax.rem(z + dz, zs), y, c))
 
-    def reader(d):
+    def reader(d, core=None):
+        at = s if core is None else sub_at(z, y, core)
         if d < 4:
-            return (g, lax.rem(s + OFFSETS[d] + rows, rows))
-        return (lax.rem(g + (1 if d == 4 else gs - 1), gs), s)
+            return (g, lax.rem(at + OFFSETS[d] + rows, rows))
+        return (lax.rem(g + (1 if d == 4 else gs - 1), gs), at)
 
     row_steps = [(dy, dc) for dy in range(ys) for dc in range(CORES) if (dy, dc) != (0, 0)]
     col_steps = list(range(1, zs))
@@ -80,9 +83,21 @@
     barrier = pltpu.get_barrier_semaphore()
     peers = [row_peer(dy, dc) for dy, dc in row_steps]
     peers += [col_peer(dz) for dz in col_steps]
-    peers += [reader(d) for d in range(DIRS)]
+    first = sub_at(z, y, 0)
+    for step in (-2, -1, 2, 3):
+        peers.append((g, lax.rem(first + step + rows, rows)))
+    for step in (1, gs - 1):
+        for core in range(CORES):
+            peers.append((lax.rem(g + step, gs), first + core))
     for peer in peers:
         pl.semaphore_signal(barrier, inc=1, device_id=peer, device_id_type=MESH)
+    small = [
+        pltpu.make_async_copy(src, dst, small_sem.at[n]) for n, (src, dst) in enumerate((
+            (basis_hbm, basis_ref), (map_hbm, map_ref), (send_hbm, send_ref), (code_hbm, code_ref),
+            (mult_hbm, mult_ref), (cinv_hbm, cinv_ref)))
+    ]
+    for copy in small:
+        copy.start()
     load_copy = pltpu.make_async_copy(load_hbm.at[0, 0], load_v, load_sem)
     load_copy.start()
     tiles = nb // TILE
@@ -95,6 +110,8 @@
         a_copy(t).start()
     s_copy = pltpu.make_async_copy(s_hbm.at[0, 0], s_v, s_sem)
     s_copy.start()
+    for copy in small:
+        copy.wait()
 
     lane = lax.broadcasted_iota(jnp.int32, (8, 128), 1)
     mine = jnp.full((8, 128), -1, jnp.int32)
@@ -102,25 +119,25 @@
         line = basis_ref[:, b * BLK:(b + 1) * BLK]
         brow[b:b + 1, :] = line
         bcol[b] = jnp.transpose(jnp.broadcast_to(line, (BLK, BLK)))
-        mine = jnp.where(lane == b, map_ref[0, b], mine)
-    mown[...] = mine
+        mine = jnp.where(lane == b, b, mine)
+        mine = jnp.where(lane == 64 + b, map_ref[0, b], mine)
     bslab[...] = jnp.zeros_like(bslab)
     for k in range(SLOTS):
         at = (k // CAP) * 8 + k % CAP
-        bslab[at:at + 1, :] = brow[pl.ds(jnp.maximum(send_ref[0, k], 0), 1), :]
-    pl.semaphore_wait(barrier, len(peers))
-
-    map_row = []
-    for n, (dy, dc) in enumerate(row_steps):
-        map_row.append(remote(mown, mrow.at[yc], ms_sem.at[n], mr_sem.at[n], row_peer(dy, dc)))
-        map_row[-1].start()
-    basis_out = []
-    for d in range(DIRS):
-        part = pl.ds(d * 8, 8)
-        basis_out.append(remote(bslab.at[part], brecv.at[part], bs_sem.at[d], br_sem.at[d], reader(d)))
-        basis_out[-1].start()
+        block = jnp.maximum(send_ref[0, k], 0)
+        mine = jnp.where(lane == PAD + at, block, mine)
+        bslab[at:at + 1, :] = brow[pl.ds(block, 1), :]
+    mown[...] = mine
+    mrow[yc] = mine
+    map_row = [
+        remote(mown, mrow.at[yc], ms_sem.at[n], mr_sem.at[n], row_peer(dy, dc))
+        for n, (dy, dc) in enumerate(row_steps)
+    ]
+    basis_out = [
+        remote(bslab.at[pl.ds(d * 8, 8)], brecv.at[pl.ds(d * 8, 8)], bs_sem.at[d], br_sem.at[d], reader(d))
+        for d in range(DIRS)
+    ]
     started += map_row + basis_out
-    mrow[yc] = mine
 
     def slab_copy(e, h, d):
         part = pl.ds(d * CAP, CAP)
@@ -130,11 +147,12 @@
             es_sem.at[n], er_sem.at[n], reader(d),
         )
 
-    def pack(e, h):
-        for d in ORDER:
-            for j in range(CAP):
-                k = d * CAP + j
-                slab[e * CH + h, k] = x[h, jnp.maximum(send_ref[0, k], 0)]
+    def fill(e, h):
+        for k in range(SLOTS):
+            slab[e * CH + h, k] = x[h, jnp.maximum(send_ref[0, k], 0)]
+
+    def send(e, h, dirs=ORDER):
+        for d in dirs:
             copy = slab_copy(e, h, d)
             copy.start()
             started.append(copy)
@@ -143,8 +161,14 @@
         for d in ORDER:
             slab_copy(e, h, d).wait_recv()
 
+    def p_fill(i, h):
+        psend[i, h] = pf[h].astype(BF)
+
+        @pl.when(c == h)
+        def _():
+            prow[i, yc] = pf[h].astype(BF)
+
     def p_send(i, h):
-        psend[i, h] = pf[h].astype(BF)
         dc = lax.rem(c + h, CORES)
         for dy in range(ys):
             n = (i * CH + h) * ys + dy
@@ -156,10 +180,6 @@
                 @pl.when(dc != 0)
                 def _():
                     copy.start()
-
-                @pl.when(dc == 0)
-                def _():
-                    prow[i, yc] = pf[h].astype(BF)
             else:
                 copy.start()
 
@@ -195,44 +215,63 @@
             q_copy(i, n, dz).start()
         pall[i, z] = prow[i]
 
+    half = PAD + DIRS * 8
+
     def partner_copy(i):
-        return remote(cout.at[i], cin.at[i], ks_sem.at[i], kr_sem.at[i], row_peer(0, 1))
+        own = pl.ds((1 - c) * half, PAD)
+        return remote(cres.at[i, own], cin.at[i], ks_sem.at[i], kr_sem.at[i], row_peer(0, 1))
+
+    def far_copy(i, core, d):
+        part = pl.ds(core * half + PAD + d * 8, 8)
+        return remote(
+            cres.at[i, part], cfar.at[i, c, pl.ds(d * 8, 8)],
+            ts_sem.at[(i * CORES + core) * DIRS + d], tr_sem.at[(i * CH + c) * DIRS + d], reader(d, core),
+        )
+
+    def far_each(i, act):
+        for d in range(DIRS):
+            for core in range(CORES):
+                if d == core:
+                    @pl.when(c == core)
+                    def _():
+                        act(far_copy(i, core, d))
+                else:
+                    act(far_copy(i, core, d))
 
     def coarse(i):
         for n, dz in enumerate(col_steps):
             q_copy(i, n, dz).wait_recv()
         every = pall[i].reshape(rows * PAD, cw)
-        crow[...] = jnp.dot(wbuf[...], every, preferred_element_type=F32).reshape(rowdev, PAD, cw)
-        cout[i] = crow[y * CORES + (1 - c)]
+        cres[i] = jnp.dot(wbuf[...], every, preferred_element_type=F32)
+        far_each(i, lambda copy: copy.start())
         partner_copy(i).start()
-
-    def t_copy(i, h, d):
-        part = pl.ds(d * 8, 8)
-        n = (i * CH + h) * DIRS + d
-        return remote(
-            cslab.at[i * CH + h, part], crecv[i * CH + h].at[part],
-            ts_sem.at[n], tr_sem.at[n], reader(d),
-        )
-
-    def spread(i, h):
+        for d in range(CORES):
+            @pl.when(c != d)
+            def _():
+                cfar[i, c, d * 8:(d + 1) * 8, :] = cres[i, pl.ds(d * half + PAD + d * 8, 8), :]
+
+    def collect(i, h):
         @pl.when(c == h)
         def _():
-            cloc[h] = crow[yc]
+            cloc[h] = cres[i, pl.ds(h * half, PAD), :]
 
         @pl.when(c != h)
         def _():
             partner_copy(i).wait_recv()
             cloc[h] = cin[i]
 
-        cslab[i * CH + h] = jnp.zeros(cslab.shape[1:], F32)
         for d in range(DIRS):
-            for j in range(CAP):
-                k = d * CAP + j
-                at = d * 8 + j
-                cslab[i * CH + h, at:at + 1, :] = cloc[h, pl.ds(jnp.maximum(send_ref[0, k], 0), 1), :]
-            copy = t_copy(i, h, d)
-            copy.start()
-            started.append(copy)
+            copy = remote(
+                cres.at[i, pl.ds(0, 8)], cfar.at[i, h, pl.ds(d * 8, 8)],
+                ts_sem.at[0], tr_sem.at[(i * CH + h) * DIRS + d], reader(d),
+            )
+            if d < CORES and d == 1 - h:
+                @pl.when(c != h)
+                def _():
+                    copy.wait_recv()
+            else:
+                copy.wait_recv()
+        cnear[h] = cfar[i, h]
 
     def code_row(b):
         code = code_ref[0, b]
@@ -272,13 +311,12 @@
     def scale(i, h):
         e = 2 * i
         wait_slabs(e, h)
-        for d in range(DIRS):
-            t_copy(i, h, d).wait_recv()
+        collect(i, h)
 
         def step(b, carry):
             code, at = code_row(b)
             own = x[h, b].astype(F32) + bcol[b] * cloc[h, pl.ds(b, 1), :]
-            far = recv[e * CH + h][code].astype(F32) + brcol[b] * crecv[i * CH + h][pl.ds(at, 1), :]
+            far = recv[e * CH + h][code].astype(F32) + brcol[b] * cnear[h, pl.ds(at, 1), :]
             sc[h, pl.ds(b * BLK, BLK), :] = ((own - far) * weight(b)).astype(BF)
             return carry
 
@@ -314,10 +352,10 @@
     def column_maps():
         for n in range(len(row_steps)):
             map_row[n].wait_recv()
-        line = lax.broadcasted_iota(jnp.int32, (8, 128), 0)
-        tile = jnp.full((8, 128), -1, jnp.int32)
+        line = lax.broadcasted_iota(jnp.int32, (rowdev, 128), 0)
+        tile = jnp.full((rowdev, 128), -1, jnp.int32)
         for n in range(rowdev):
-            tile = jnp.where(line == n, mrow[n], tile)
+            tile = jnp.where(line == n, mrow[n, 0:rowdev], tile)
         mtile[...] = tile
         copies = []
         for n, dz in enumerate(col_steps):
@@ -327,19 +365,21 @@
         started.extend(copies)
         return copies
 
+    shift_row = (rowdev * PAD).bit_length() - 1
+    shift_pad = PAD.bit_length() - 1
+
+    def mark(dst, dofs):
+        grid = jnp.transpose(dofs.astype(F32))[64:64 + PAD]
+        width = dst.shape[1]
+        ids = lax.broadcasted_iota(jnp.int32, (PAD, width), 1).astype(F32)
+        for n in range(rows):
+            hit = jnp.broadcast_to(grid[:, n:n + 1], (PAD, width)) == ids
+            dst[n * PAD:(n + 1) * PAD, :] = jnp.where(hit, 1.0, 0.0).astype(BF)
+
     def columns(copies):
         for copy in copies:
             copy.wait_recv()
-        grid = jnp.transpose(mall[...].reshape(zs * 8, 128).astype(F32))
-        order = rows * PAD
-        width = onehot.shape[1]
-        ids = lax.broadcasted_iota(jnp.int32, (PAD, width), 1).astype(F32)
-        for zz in range(zs):
-            for r in range(rowdev):
-                at = (zz * rowdev + r) * PAD
-                n = zz * 8 + r
-                hit = jnp.broadcast_to(grid[:PAD, n:n + 1], (PAD, width)) == ids
-                onehot[at:at + PAD, :] = jnp.where(hit, 1.0, 0.0).astype(BF)
+        mark(onehot, mall[...].reshape(rows, 128))
         picked = lax.dot_general(
             cinv_ref[0].astype(BF), onehot[...], (((1,), (1,)), ((), ())), preferred_element_type=F32
         ).astype(BF)
@@ -355,67 +395,103 @@
         started.extend(copies)
         return copies
 
+    def mark_rows():
+        dofs = mall[...].reshape(rows, 128)
+        high = lax.shift_right_logical(dofs, shift_row)
+        mid = lax.shift_right_logical(dofs, shift_pad) & (rowdev - 1)
+        moved = mid * (zs * PAD) + high * PAD + (dofs & (PAD - 1))
+        mark(twohot, jnp.where(dofs >= 0, moved, -1))
+
     def share_columns(copies):
         for copy in copies:
             copy.wait_recv()
+        turned = jnp.transpose(colz[...].reshape(zs * PAD, rowdev * PAD).astype(F32)).astype(BF)
+        colt[...] = turned.reshape(ys, CORES * PAD, zs * PAD)
         out = []
         for n, (dy, dc) in enumerate(row_steps):
-            out.append(remote(colz, colall.at[:, yc], ys_sem.at[n], yr_sem.at[n], row_peer(dy, dc)))
+            out.append(remote(
+                colt.at[lax.rem(y + dy, ys)], colall.at[yc], ys_sem.at[n], yr_sem.at[n], row_peer(dy, dc)
+            ))
             out[-1].start()
-        colall[:, yc] = colz[...]
+        colall[yc] = colt[y]
         started.extend(out)
         return out
 
     def coarse_rows(copies):
+        width = CORES * PAD
+        ids = lax.broadcasted_iota(jnp.int32, (half, width), 1).astype(F32)
+        parts = []
+        for core in range(CORES):
+            table = jnp.broadcast_to(mrow[y * CORES + core, 0:1].astype(F32), (128, 128))
+            want = jnp.transpose(table)[:half, :width]
+            want = jnp.where(want >= 0, want + core * PAD, -1.0)
+            parts.append(jnp.where(want == ids, 1.0, 0.0))
+        wanted = jnp.concatenate(parts, axis=0).astype(BF)
         for copy in copies:
             copy.wait_recv()
-        mat = colall[...].reshape(onehot.shape[1], rowdev * PAD)
-        wide = jnp.dot(onehot[...], mat, preferred_element_type=F32)
-        wbuf[...] = jnp.transpose(wide).astype(BF)
+        mat = jnp.concatenate([colall[n] for n in range(rowdev)], axis=1)
+        both = lax.dot_general(
+            mat, twohot[...], (((1,), (1,)), ((), ())), preferred_element_type=F32
+        ).astype(BF)
+        wbuf[...] = jnp.dot(wanted, both, preferred_element_type=F32).astype(BF)
 
     pf[...] = jnp.zeros_like(pf)
     first_solve()
     for h in range(CH):
+        p_fill(0, h)
+        fill(0, h)
+    pl.semaphore_wait(barrier, len(peers))
+    for copy in map_row:
+        copy.start()
+    for h in range(CH):
         p_send(0, h)
-    for h in range(CH):
-        pack(0, h)
+    for copy in basis_out:
+        copy.start()
+    for h in range(CH):
+        send(0, h, ACROSS)
     map_col = column_maps()
     relay(0)
+    send(0, 0, ALONG)
+    col_out = columns(map_col)
+    mark_rows()
     for copy in basis_out:
         copy.wait_recv()
     for b in range(nblk):
         _, at = code_row(b)
         brcol[b] = jnp.transpose(jnp.broadcast_to(brecv[pl.ds(at, 1), :], (BLK, BLK)))
-    col_out = columns(map_col)
     row_out = share_columns(col_out)
+    send(0, 1, ALONG)
     coarse_rows(row_out)
     coarse(0)
-    for h in range(CH):
-        spread(0, h)
     s_copy.wait()
     for h in range(CH):
         scale(0, h)
         dirichlet(h)
-        pack(1, h)
+        fill(1, h)
+        send(1, h)
     for h in range(CH):
         update(0, h)
         solve(h)
+        p_fill(1, h)
         p_send(1, h)
-        pack(2, h)
+        fill(2, h)
+        send(2, h, ACROSS)
 
         @pl.when(c == h)
         def _():
             relay(1)
 
+        send(2, h, ALONG)
+
     for h in range(CH):
         @pl.when(c == h)
         def _():
             coarse(1)
 
-        spread(1, h)
         scale(1, h)
         dirichlet(h)
-        pack(3, h)
+        fill(3, h)
+        send(3, h)
     outs = []
     for h in range(CH):
         update(1, h)
@@ -430,6 +506,7 @@
         for n, dz in enumerate(col_steps):
             q_copy(i, n, dz).wait_send()
         partner_copy(i).wait_send()
+        far_each(i, lambda copy: copy.wait_send())
     for copy in outs:
         copy.wait()
 
@@ -447,16 +524,21 @@
     dma = pltpu.SemaphoreType.DMA
     vm = pltpu.VMEM
     exchanges = 2 * ITERS * CH
+    half = PAD + DIRS * 8
+    sm = pltpu.SMEM
     scratch = [
+        vm((1, nb), F32), vm((1, own, nc), F32), sm((1, nblk), jnp.int32), sm((1, nblk), jnp.int32),
+        sm((1, nblk), jnp.int32), sm((1, SLOTS), jnp.int32), dma((6,)),
         vm((nb, cases), BF), vm((nb, nb), BF), vm((nb, nb), BF),
         dma, dma((tiles,)), dma, dma((CH,)),
         vm((nblk, BLK, BLK), F32), vm((nblk, BLK, BLK), F32), vm((PAD, BLK), F32),
         vm((DIRS * 8, BLK), F32), vm((DIRS * 8, BLK), F32), dma((DIRS,)), dma((DIRS,)),
-        vm((8, 128), jnp.int32), vm((rowdev, 8, 128), jnp.int32), vm((8, 128), jnp.int32),
-        vm((zs, 8, 128), jnp.int32), dma((rowdev,)), dma((rowdev,)), dma((zs,)), dma((zs,)),
-        vm((rows * PAD, nc), BF), vm((zs, own, rowdev * PAD), BF), vm((zs, own, rowdev * PAD), BF),
-        vm((zs, rowdev, own, rowdev * PAD), BF),
-        dma((zs,)), dma((zs,)), dma((rowdev,)), dma((rowdev,)), vm((rowdev * PAD, rows * PAD), BF),
+        vm((8, 128), jnp.int32), vm((rowdev, 8, 128), jnp.int32), vm((rowdev, 128), jnp.int32),
+        vm((zs, rowdev, 128), jnp.int32), dma((rowdev,)), dma((rowdev,)), dma((zs,)), dma((zs,)),
+        vm((rows * PAD, nc), BF), vm((rows * PAD, nc), BF),
+        vm((zs, own, rowdev * PAD), BF), vm((zs, own, rowdev * PAD), BF),
+        vm((ys, CORES * PAD, zs * own), BF), vm((rowdev, CORES * PAD, zs * own), BF),
+        dma((zs,)), dma((zs,)), dma((rowdev,)), dma((rowdev,)), vm((CORES * half, rows * PAD), BF),
         vm((CH, nblk, BLK, cw), BF), vm((exchanges, SLOTS, BLK, cw), BF),
         *[vm((SLOTS, BLK, cw), BF) for _ in range(exchanges)],
         dma((exchanges * DIRS,)), dma((exchanges * DIRS,)),
@@ -464,19 +546,15 @@
         vm((CH, PAD, cw), F32), vm((ITERS, CH, PAD, cw), BF), vm((ITERS, rowdev, PAD, cw), BF),
         vm((ITERS, zs, rowdev, PAD, cw), BF),
         dma((ITERS * CH * ys,)), dma((ITERS * rowdev,)), dma((ITERS * zs,)), dma((ITERS * zs,)),
-        vm((rowdev, PAD, cw), F32), vm((ITERS, PAD, cw), F32), vm((ITERS, PAD, cw), F32),
-        vm((CH, PAD, cw), F32), dma((ITERS,)), dma((ITERS,)),
-        vm((ITERS * CH, DIRS * 8, cw), F32),
-        *[vm((DIRS * 8, cw), F32) for _ in range(ITERS * CH)],
-        dma((ITERS * CH * DIRS,)), dma((ITERS * CH * DIRS,)),
+        vm((ITERS, CORES * half, cw), F32), vm((ITERS, PAD, cw), F32), vm((CH, PAD, cw), F32),
+        vm((ITERS, CH, DIRS * 8, cw), F32), vm((CH, DIRS * 8, cw), F32), dma((ITERS,)), dma((ITERS,)),
+        dma((ITERS * CORES * DIRS,)), dma((ITERS * CH * DIRS,)),
     ]
     hbm = pl.BlockSpec(memory_space=pl.ANY)
-    inside = pl.BlockSpec(memory_space=pltpu.VMEM)
-    scalars = pl.BlockSpec(memory_space=pltpu.SMEM)
     return pl.pallas_call(
         functools.partial(kernel, zs, ys, gs),
         out_shape=jax.ShapeDtypeStruct(load_cases.shape, F32),
-        in_specs=[hbm, hbm, hbm, inside, inside, scalars, scalars, scalars, scalars],
+        in_specs=[hbm] * 9,
         out_specs=hbm,
         scratch_shapes=scratch,
         compiler_params=pltpu.CompilerParams(

time: 98.3 us -> 97.8 us (level); the launches traced: 97.1 us -> 97.7 us
  no operation moved by 1% of the time
where the time goes in v2:
time: 97.8 us; the launch traced here: 97.7 us
  Pallas kernels  95.1 us (97%)
  local copies, waits for them, and re-layouts  2.65 us (3%)
    pallas_call x1, Pallas kernels, on_device(): pl.pallas_call(functools.partial(kernel, zs, ys, gs), out_shape=jax.Shape...  95.1 us
    unnamed x1, local copies, waits for them, and re-layouts  2.65 us

profile of v2, /device:TPU:1, one launch (start us, length us, event | category | flops | bytes accessed | tf_op | source)
XLA Modules:
  0.0 97.7 jit_solution(85059416626868975)
XLA Ops:
  0.0 95.1 %feti.1 = f32[1,1,1536,256]{3,2,1,0:T(8,128)} custom-call(bf16[1,1,1536,256]{3,2,1,0:T(8,128)(2,1)} %load_hbm.1, bf16[1,1,1536,1536]{3,2,1,0:T(8,128)(2,1)} %a_hbm.1, bf16[1,1,1536,1536]{3,2,1,0:T(8,128)(2,1)} %s_hbm.1, f32[1,1536]{1,0:T(1,128)} %bitcast.5, f32[1,16,1024]{2,1,0:T(8,128)} %cinv_hbm.1, s32[1,12]{1,0:T(1,128)} %bitcast.6, s32[1,12]{1,0:T(1,128)} %bitcast.7, ...), custom_call_target="tpu_custom_call" | custom-call | tf_op jit(solution)/shard_map/feti/pallas_call | solution.py:554
  95.1 2.7 %copy.11 = f32[1,1,1536,256]{3,2,1,0:T(8,128)} copy(f32[1,1,1536,256]{3,2,1,0:T(8,128)} %feti.1) | data formatting | bytes 3145728

commit v3 on v2

--- a/solution.py
+++ b/solution.py
@@ -56,19 +56,30 @@
     def sub_at(zz, yy, cc):
         return (zz * ys + yy) * CORES + cc
 
+    row_ids = [[(g, sub_at(z, lax.rem(y + dy, ys), cc)) for cc in (c, 1 - c)] for dy in range(ys)]
+    col_ids = [(g, sub_at(lax.rem(z + dz, zs), y, c)) for dz in range(zs)]
+    near = {step: lax.rem(s - c + step + rows, rows) for step in (-2, -1, 0, 1, 2, 3)}
+    sides = [lax.rem(g + step, gs) for step in (1, gs - 1)]
+
+    def reader_of(at, core, d):
+        return (g, at(core + OFFSETS[d])) if d < 4 else (sides[d - 4], at(core))
+
+    core_readers = [[reader_of(lambda step: near[step], core, d) for d in range(DIRS)] for core in range(CORES)]
+    own_readers = [
+        (jnp.where(c == 0, a[0], b[0]), jnp.where(c == 0, a[1], b[1])) for a, b in zip(*core_readers)
+    ]
+
     def row_peer(dy, dc):
-        yy = lax.rem(y + dy, ys)
-        cc = lax.rem(c + dc, CORES)
-        return (g, sub_at(z, yy, cc))
+        if isinstance(dc, int):
+            return row_ids[dy][dc]
+        here, there = row_ids[dy]
+        return (g, jnp.where(dc == 0, here[1], there[1]))
 
     def col_peer(dz):
-        return (g, sub_at(lax.rem(z + dz, zs), y, c))
+        return col_ids[dz]
 
     def reader(d, core=None):
-        at = s if core is None else sub_at(z, y, core)
-        if d < 4:
-            return (g, lax.rem(at + OFFSETS[d] + rows, rows))
-        return (lax.rem(g + (1 if d == 4 else gs - 1), gs), at)
+        return own_readers[d] if core is None else core_readers[core][d]
 
     row_steps = [(dy, dc) for dy in range(ys) for dc in range(CORES) if (dy, dc) != (0, 0)]
     col_steps = list(range(1, zs))
@@ -83,12 +94,8 @@
     barrier = pltpu.get_barrier_semaphore()
     peers = [row_peer(dy, dc) for dy, dc in row_steps]
     peers += [col_peer(dz) for dz in col_steps]
-    first = sub_at(z, y, 0)
-    for step in (-2, -1, 2, 3):
-        peers.append((g, lax.rem(first + step + rows, rows)))
-    for step in (1, gs - 1):
-        for core in range(CORES):
-            peers.append((lax.rem(g + step, gs), first + core))
+    peers += [(g, near[step]) for step in (-2, -1, 2, 3)]
+    peers += [(side, near[core]) for side in sides for core in range(CORES)]
     for peer in peers:
         pl.semaphore_signal(barrier, inc=1, device_id=peer, device_id_type=MESH)
     small = [
@@ -300,13 +307,9 @@
         lax.fori_loop(0, tiles, step, 0)
 
     def solve(h):
-        def step(t, carry):
-            acc = jnp.dot(a_v[pl.ds(t * TILE, TILE), :], res[h], preferred_element_type=F32)
-            for i in range(per):
-                keep(t * per + i, h, acc[i * BLK:(i + 1) * BLK])
-            return carry
-
-        lax.fori_loop(0, tiles, step, 0)
+        acc = jnp.dot(a_v[...], res[h], preferred_element_type=F32)
+        for b in range(nblk):
+            keep(b, h, acc[b * BLK:(b + 1) * BLK])
 
     def scale(i, h):
         e = 2 * i
@@ -323,14 +326,9 @@
         lax.fori_loop(0, nblk, step, 0)
 
     def dirichlet(h):
-        def step(t, carry):
-            acc = jnp.dot(s_v[pl.ds(t * TILE, TILE), :], sc[h], preferred_element_type=F32)
-            for i in range(per):
-                b = t * per + i
-                x[h, b] = (acc[i * BLK:(i + 1) * BLK] * weight(b)).astype(BF)
-            return carry
-
-        lax.fori_loop(0, tiles, step, 0)
+        acc = jnp.dot(s_v[...], sc[h], preferred_element_type=F32)
+        for b in range(nblk):
+            x[h, b] = (acc[b * BLK:(b + 1) * BLK] * weight(b)).astype(BF)
 
     def update(i, h):
         e = 2 * i + 1
@@ -448,11 +446,10 @@
     for copy in basis_out:
         copy.start()
     for h in range(CH):
-        send(0, h, ACROSS)
+        send(0, h)
     map_col = column_maps()
+    col_out = columns(map_col)
     relay(0)
-    send(0, 0, ALONG)
-    col_out = columns(map_col)
     mark_rows()
     for copy in basis_out:
         copy.wait_recv()
@@ -460,7 +457,6 @@
         _, at = code_row(b)
         brcol[b] = jnp.transpose(jnp.broadcast_to(brecv[pl.ds(at, 1), :], (BLK, BLK)))
     row_out = share_columns(col_out)
-    send(0, 1, ALONG)
     coarse_rows(row_out)
     coarse(0)
     s_copy.wait()
@@ -475,13 +471,11 @@
         p_fill(1, h)
         p_send(1, h)
         fill(2, h)
-        send(2, h, ACROSS)
+        send(2, h)
 
         @pl.when(c == h)
         def _():
             relay(1)
-
-        send(2, h, ALONG)
 
     for h in range(CH):
         @pl.when(c == h)

time: 97.8 us -> 93.4 us (0.955)
  Pallas kernels: 95.1 us -> 90.6 us
    pallas_call x1, Pallas kernels: 95.1 us -> 90.6 us  [on_device(): pl.pallas_call(functools.partial(kernel, zs, ys, gs), out_shape=jax.Shape...]
where the time goes in v3:
time: 93.4 us; the launch traced here: 93.2 us
  Pallas kernels  90.6 us (97%)
  local copies, waits for them, and re-layouts  2.65 us (3%)
    pallas_call x1, Pallas kernels, on_device(): pl.pallas_call(functools.partial(kernel, zs, ys, gs), out_shape=jax.Shape...  90.6 us
    unnamed x1, local copies, waits for them, and re-layouts  2.65 us

profile of v3, /device:TPU:1, one launch (start us, length us, event | category | flops | bytes accessed | tf_op | source)
XLA Modules:
  0.0 93.2 jit_solution(17955289713644144845)
XLA Ops:
  0.0 90.6 %feti.1 = f32[1,1,1536,256]{3,2,1,0:T(8,128)} custom-call(bf16[1,1,1536,256]{3,2,1,0:T(8,128)(2,1)} %load_hbm.1, bf16[1,1,1536,1536]{3,2,1,0:T(8,128)(2,1)} %a_hbm.1, bf16[1,1,1536,1536]{3,2,1,0:T(8,128)(2,1)} %s_hbm.1, f32[1,1536]{1,0:T(1,128)} %bitcast.5, f32[1,16,1024]{2,1,0:T(8,128)} %cinv_hbm.1, s32[1,12]{1,0:T(1,128)} %bitcast.6, s32[1,12]{1,0:T(1,128)} %bitcast.7, ...), custom_call_target="tpu_custom_call" | custom-call | tf_op jit(solution)/shard_map/feti/pallas_call | solution.py:548
  90.6 2.7 %copy.11 = f32[1,1,1536,256]{3,2,1,0:T(8,128)} copy(f32[1,1,1536,256]{3,2,1,0:T(8,128)} %feti.1) | data formatting | bytes 3145728

commit v4 on v3

--- a/solution.py
+++ b/solution.py
@@ -15,6 +15,7 @@
 PAD = 16
 CH = 2
 CORES = 2
+TERMS = 2 * PAD
 TILE = 256
 OFFSETS = (1, -1, 2, -2)
 ALONG = (2, 3, 0, 1)
@@ -31,13 +32,14 @@
     out_hbm,
     basis_ref, cinv_ref, map_ref, mult_ref, code_ref, send_ref, small_sem,
     load_v, a_v, s_v, load_sem, a_sem, s_sem, out_sem,
-    bcol, brcol, brow, bslab, brecv, bs_sem, br_sem,
+    bcol, brow, bslab, brecv, bs_sem, br_sem,
     mown, mrow, mtile, mall, ms_sem, mr_sem, zs_sem, zr_sem,
     onehot, twohot, selbuf, colz, colt, colall, cs_sem, cr_sem, ys_sem, yr_sem, wbuf,
     x, slab, rv0, rv1, rv2, rv3, rv4, rv5, rv6, rv7, es_sem, er_sem,
     sc, mul, res,
     pf, psend, prow, pall, ps_sem, pr_sem, qs_sem, qr_sem,
     cres, cin, cloc, cfar, cnear, ks_sem, kr_sem, ts_sem, tr_sem,
+    dmat, gt, gslab, grecv, gs_sem, gr_sem, gg, ccf, ccs, ccr, call, us_sem, ur_sem,
 ):
     nb, cases = load_v.shape
     nblk = nb // BLK
@@ -314,16 +316,71 @@
     def scale(i, h):
         e = 2 * i
         wait_slabs(e, h)
+
+        def step(b, carry):
+            code, _ = code_row(b)
+            diff = x[h, b].astype(F32) - recv[e * CH + h][code].astype(F32)
+            sc[h, pl.ds(b * BLK, BLK), :] = (diff * weight(b)).astype(BF)
+            return carry
+
+        lax.fori_loop(0, nblk, step, 0)
+
+    def response():
+        for copy in basis_out:
+            copy.wait_recv()
+        lanes = lax.broadcasted_iota(jnp.int32, (BLK, BLK), 1)
+        for b in range(nblk):
+            _, at = code_row(b)
+            far = jnp.transpose(jnp.broadcast_to(brecv[pl.ds(at, 1), :], (BLK, BLK)))
+            both = jnp.where(lanes == b, bcol[b], jnp.where(lanes == PAD + b, -far, 0.0))
+            dmat[b * BLK:(b + 1) * BLK, :] = (both * weight(b)).astype(BF)
+        s_copy.wait()
+        acc = jnp.dot(s_v[...], dmat[...], preferred_element_type=F32)
+        for b in range(nblk):
+            turned = jnp.transpose(acc[b * BLK:(b + 1) * BLK] * weight(b))
+            gt[b] = turned[:TERMS].astype(BF)
+        for k in range(SLOTS):
+            gslab[k] = gt[jnp.maximum(send_ref[0, k], 0)]
+        copies = []
+        for d in ORDER:
+            part = pl.ds(d * CAP, CAP)
+            copies.append(remote(gslab.at[part], grecv.at[part], gs_sem.at[d], gr_sem.at[d], reader(d)))
+            copies[-1].start()
+        started.extend(copies)
+        return copies
+
+    def responses(copies):
+        for copy in copies:
+            copy.wait_recv()
+        rest = jnp.zeros((2 * BLK - (1 + DIRS) * TERMS, BLK), F32)
+        for b in range(nblk):
+            code, _ = code_row(b)
+            far = -grecv[code].astype(F32)
+            source = jnp.full(far.shape, code // CAP, jnp.int32)
+            pieces = [gt[b].astype(F32)]
+            pieces += [jnp.where(source == d, far, 0.0) for d in range(DIRS)] + [rest]
+            wide = jnp.concatenate(pieces, axis=0)
+            gg[b * BLK:(b + 1) * BLK, :BLK] = jnp.transpose(wide[:BLK]).astype(BF)
+            gg[b * BLK:(b + 1) * BLK, BLK:] = jnp.transpose(wide[BLK:]).astype(BF)
+
+    def cc_copy(i, h, d):
+        n = i * CH + h
+        return remote(
+            ccs.at[n], ccr.at[n, d], us_sem.at[n * DIRS + d], ur_sem.at[n * DIRS + d], reader(d)
+        )
+
+    def cc_send(i, h):
         collect(i, h)
-
-        def step(b, carry):
-            code, at = code_row(b)
-            own = x[h, b].astype(F32) + bcol[b] * cloc[h, pl.ds(b, 1), :]
-            far = recv[e * CH + h][code].astype(F32) + brcol[b] * cnear[h, pl.ds(at, 1), :]
-            sc[h, pl.ds(b * BLK, BLK), :] = ((own - far) * weight(b)).astype(BF)
-            return carry
-
-        lax.fori_loop(0, nblk, step, 0)
+        ccf[...] = jnp.zeros_like(ccf)
+        ccf[0:PAD, :] = cloc[h]
+        for b in range(nblk):
+            _, at = code_row(b)
+            ccf[PAD + b:PAD + b + 1, :] = cnear[h, pl.ds(at, 1), :]
+        ccs[i * CH + h] = ccf[...].astype(BF)
+        for d in ORDER:
+            copy = cc_copy(i, h, d)
+            copy.start()
+            started.append(copy)
 
     def dirichlet(h):
         acc = jnp.dot(s_v[...], sc[h], preferred_element_type=F32)
@@ -333,19 +390,20 @@
     def update(i, h):
         e = 2 * i + 1
         wait_slabs(e, h)
+        for d in range(DIRS):
+            cc_copy(i, h, d).wait_recv()
+            call[(d + 1) * TERMS:(d + 2) * TERMS, :] = ccr[i * CH + h, d]
+        call[:TERMS, :] = ccs[i * CH + h]
+        extra = jnp.dot(gg[...], call[...], preferred_element_type=F32)
         cols = slice(h * cw, (h + 1) * cw)
-
-        def step(b, carry):
-            part = pl.ds(b * BLK, BLK)
-            new = x[h, b].astype(F32) - recv[e * CH + h][code_ref[0, b]].astype(F32)
+        for b in range(nblk):
+            part = slice(b * BLK, (b + 1) * BLK)
+            new = x[h, b].astype(F32) - recv[e * CH + h][code_ref[0, b]].astype(F32) + extra[part]
             if i == 0:
                 res[h, part, :] = (load_v[part, cols].astype(F32) - new).astype(BF)
             else:
                 new = mul[part, cols] + new
             mul[part, cols] = new
-            return carry
-
-        lax.fori_loop(0, nblk, step, 0)
 
     def column_maps():
         for n in range(len(row_steps)):
@@ -434,6 +492,7 @@
         wbuf[...] = jnp.dot(wanted, both, preferred_element_type=F32).astype(BF)
 
     pf[...] = jnp.zeros_like(pf)
+    call[...] = jnp.zeros_like(call)
     first_solve()
     for h in range(CH):
         p_fill(0, h)
@@ -445,47 +504,47 @@
         p_send(0, h)
     for copy in basis_out:
         copy.start()
-    for h in range(CH):
-        send(0, h)
+    send(0, 0)
     map_col = column_maps()
+    send(0, 1)
     col_out = columns(map_col)
     relay(0)
     mark_rows()
-    for copy in basis_out:
-        copy.wait_recv()
-    for b in range(nblk):
-        _, at = code_row(b)
-        brcol[b] = jnp.transpose(jnp.broadcast_to(brecv[pl.ds(at, 1), :], (BLK, BLK)))
     row_out = share_columns(col_out)
+    gain = response()
+    scale(0, 0)
+    dirichlet(0)
+    fill(1, 0)
+    send(1, 0)
     coarse_rows(row_out)
     coarse(0)
-    s_copy.wait()
+    scale(0, 1)
+    dirichlet(1)
+    fill(1, 1)
     for h in range(CH):
-        scale(0, h)
-        dirichlet(h)
-        fill(1, h)
-        send(1, h)
+        cc_send(0, h)
+    send(1, 1)
+    responses(gain)
     for h in range(CH):
         update(0, h)
         solve(h)
         p_fill(1, h)
         p_send(1, h)
         fill(2, h)
+    for h in range(CH):
         send(2, h)
-
-        @pl.when(c == h)
-        def _():
-            relay(1)
-
+    relay(1)
+    scale(1, 0)
+    dirichlet(0)
+    fill(3, 0)
+    send(3, 0)
+    coarse(1)
+    scale(1, 1)
+    dirichlet(1)
+    fill(3, 1)
     for h in range(CH):
-        @pl.when(c == h)
-        def _():
-            coarse(1)
-
-        scale(1, h)
-        dirichlet(h)
-        fill(3, h)
-        send(3, h)
+        cc_send(1, h)
+    send(3, 1)
     outs = []
     for h in range(CH):
         update(1, h)
@@ -525,7 +584,7 @@
         sm((1, nblk), jnp.int32), sm((1, SLOTS), jnp.int32), dma((6,)),
         vm((nb, cases), BF), vm((nb, nb), BF), vm((nb, nb), BF),
         dma, dma((tiles,)), dma, dma((CH,)),
-        vm((nblk, BLK, BLK), F32), vm((nblk, BLK, BLK), F32), vm((PAD, BLK), F32),
+        vm((nblk, BLK, BLK), F32), vm((PAD, BLK), F32),
         vm((DIRS * 8, BLK), F32), vm((DIRS * 8, BLK), F32), dma((DIRS,)), dma((DIRS,)),
         vm((8, 128), jnp.int32), vm((rowdev, 8, 128), jnp.int32), vm((rowdev, 128), jnp.int32),
         vm((zs, rowdev, 128), jnp.int32), dma((rowdev,)), dma((rowdev,)), dma((zs,)), dma((zs,)),
@@ -543,6 +602,10 @@
         vm((ITERS, CORES * half, cw), F32), vm((ITERS, PAD, cw), F32), vm((CH, PAD, cw), F32),
         vm((ITERS, CH, DIRS * 8, cw), F32), vm((CH, DIRS * 8, cw), F32), dma((ITERS,)), dma((ITERS,)),
         dma((ITERS * CORES * DIRS,)), dma((ITERS * CH * DIRS,)),
+        vm((nb, BLK), BF), vm((nblk, TERMS, BLK), BF), vm((SLOTS, TERMS, BLK), BF), vm((SLOTS, TERMS, BLK), BF),
+        dma((DIRS,)), dma((DIRS,)), vm((nb, 2 * BLK), BF), vm((TERMS, cw), F32), vm((ITERS * CH, TERMS, cw), BF),
+        vm((ITERS * CH, DIRS, TERMS, cw), BF), vm((2 * BLK, cw), BF),
+        dma((ITERS * CH * DIRS,)), dma((ITERS * CH * DIRS,)),
     ]
     hbm = pl.BlockSpec(memory_space=pl.ANY)
     return pl.pallas_call(

time: 93.4 us -> 90.2 us (0.966)
  Pallas kernels: 90.6 us -> 86.7 us
    pallas_call x1, Pallas kernels: 90.6 us -> 86.7 us  [on_device(): pl.pallas_call(functools.partial(kernel, zs, ys, gs), out_shape=jax.Shape...]
where the time goes in v4:
time: 90.2 us; the launch traced here: 89.4 us
  Pallas kernels  86.7 us (96%)
  local copies, waits for them, and re-layouts  2.65 us (3%)
    pallas_call x1, Pallas kernels, on_device(): pl.pallas_call(functools.partial(kernel, zs, ys, gs), out_shape=jax.Shape...  86.7 us
    unnamed x1, local copies, waits for them, and re-layouts  2.65 us

profile of v4, /device:TPU:1, one launch (start us, length us, event | category | flops | bytes accessed | tf_op | source)
XLA Modules:
  0.0 89.4 jit_solution(16113723894646678101)
XLA Ops:
  0.0 86.7 %feti.1 = f32[1,1,1536,256]{3,2,1,0:T(8,128)} custom-call(bf16[1,1,1536,256]{3,2,1,0:T(8,128)(2,1)} %load_hbm.1, bf16[1,1,1536,1536]{3,2,1,0:T(8,128)(2,1)} %a_hbm.1, bf16[1,1,1536,1536]{3,2,1,0:T(8,128)(2,1)} %s_hbm.1, f32[1,1536]{1,0:T(1,128)} %bitcast.5, f32[1,16,1024]{2,1,0:T(8,128)} %cinv_hbm.1, s32[1,12]{1,0:T(1,128)} %bitcast.6, s32[1,12]{1,0:T(1,128)} %bitcast.7, ...), custom_call_target="tpu_custom_call" | custom-call | tf_op jit(solution)/shard_map/feti/pallas_call | solution.py:611
  86.7 2.7 %copy.11 = f32[1,1,1536,256]{3,2,1,0:T(8,128)} copy(f32[1,1,1536,256]{3,2,1,0:T(8,128)} %feti.1) | data formatting | bytes 3145728

commit v5 on v4

--- a/solution.py
+++ b/solution.py
@@ -334,7 +334,6 @@
             far = jnp.transpose(jnp.broadcast_to(brecv[pl.ds(at, 1), :], (BLK, BLK)))
             both = jnp.where(lanes == b, bcol[b], jnp.where(lanes == PAD + b, -far, 0.0))
             dmat[b * BLK:(b + 1) * BLK, :] = (both * weight(b)).astype(BF)
-        s_copy.wait()
         acc = jnp.dot(s_v[...], dmat[...], preferred_element_type=F32)
         for b in range(nblk):
             turned = jnp.transpose(acc[b * BLK:(b + 1) * BLK] * weight(b))
@@ -507,23 +506,24 @@
     send(0, 0)
     map_col = column_maps()
     send(0, 1)
-    col_out = columns(map_col)
-    relay(0)
-    mark_rows()
-    row_out = share_columns(col_out)
-    gain = response()
+    s_copy.wait()
     scale(0, 0)
     dirichlet(0)
     fill(1, 0)
+    col_out = columns(map_col)
+    relay(0)
     send(1, 0)
-    coarse_rows(row_out)
-    coarse(0)
+    mark_rows()
+    row_out = share_columns(col_out)
     scale(0, 1)
     dirichlet(1)
     fill(1, 1)
+    send(1, 1)
+    gain = response()
+    coarse_rows(row_out)
+    coarse(0)
     for h in range(CH):
         cc_send(0, h)
-    send(1, 1)
     responses(gain)
     for h in range(CH):
         update(0, h)
@@ -542,9 +542,9 @@
     scale(1, 1)
     dirichlet(1)
     fill(3, 1)
+    send(3, 1)
     for h in range(CH):
         cc_send(1, h)
-    send(3, 1)
     outs = []
     for h in range(CH):
         update(1, h)

time: 90.2 us -> 89 us (0.987)
  no operation moved by 1% of the time
where the time goes in v5:
time: 89 us; the launch traced here: 88.9 us
  Pallas kernels  86.2 us (97%)
  local copies, waits for them, and re-layouts  2.65 us (3%)
    pallas_call x1, Pallas kernels, on_device(): pl.pallas_call(functools.partial(kernel, zs, ys, gs), out_shape=jax.Shape...  86.2 us
    unnamed x1, local copies, waits for them, and re-layouts  2.65 us

profile of v5, /device:TPU:1, one launch (start us, length us, event | category | flops | bytes accessed | tf_op | source)
XLA Modules:
  0.0 88.9 jit_solution(7043413495929005704)
XLA Ops:
  0.0 86.2 %feti.1 = f32[1,1,1536,256]{3,2,1,0:T(8,128)} custom-call(bf16[1,1,1536,256]{3,2,1,0:T(8,128)(2,1)} %load_hbm.1, bf16[1,1,1536,1536]{3,2,1,0:T(8,128)(2,1)} %a_hbm.1, bf16[1,1,1536,1536]{3,2,1,0:T(8,128)(2,1)} %s_hbm.1, f32[1,1536]{1,0:T(1,128)} %bitcast.5, f32[1,16,1024]{2,1,0:T(8,128)} %cinv_hbm.1, s32[1,12]{1,0:T(1,128)} %bitcast.6, s32[1,12]{1,0:T(1,128)} %bitcast.7, ...), custom_call_target="tpu_custom_call" | custom-call | tf_op jit(solution)/shard_map/feti/pallas_call | solution.py:611
  86.2 2.7 %copy.11 = f32[1,1,1536,256]{3,2,1,0:T(8,128)} copy(f32[1,1,1536,256]{3,2,1,0:T(8,128)} %feti.1) | data formatting | bytes 3145728

commit v6 on v5

--- a/solution.py
+++ b/solution.py
@@ -503,25 +503,27 @@
         p_send(0, h)
     for copy in basis_out:
         copy.start()
-    send(0, 0)
+    for h in range(CH):
+        send(0, h, ACROSS)
     map_col = column_maps()
-    send(0, 1)
+    send(0, 0, ALONG)
+    col_out = columns(map_col)
+    relay(0)
+    send(0, 1, ALONG)
+    mark_rows()
     s_copy.wait()
     scale(0, 0)
     dirichlet(0)
     fill(1, 0)
-    col_out = columns(map_col)
-    relay(0)
+    row_out = share_columns(col_out)
     send(1, 0)
-    mark_rows()
-    row_out = share_columns(col_out)
     scale(0, 1)
     dirichlet(1)
     fill(1, 1)
     send(1, 1)
-    gain = response()
     coarse_rows(row_out)
     coarse(0)
+    gain = response()
     for h in range(CH):
         cc_send(0, h)
     responses(gain)
@@ -531,9 +533,9 @@
         p_fill(1, h)
         p_send(1, h)
         fill(2, h)
-    for h in range(CH):
-        send(2, h)
+        send(2, h, ORDER if h == 0 else ACROSS)
     relay(1)
+    send(2, 1, ALONG)
     scale(1, 0)
     dirichlet(0)
     fill(3, 0)

time: 89 us -> 88.9 us (level)
  no operation moved by 1% of the time
where the time goes in v6:
time: 88.9 us; the launch traced here: 88.8 us
  Pallas kernels  86.1 us (97%)
  local copies, waits for them, and re-layouts  2.65 us (3%)
    pallas_call x1, Pallas kernels, on_device(): pl.pallas_call(functools.partial(kernel, zs, ys, gs), out_shape=jax.Shape...  86.1 us
    unnamed x1, local copies, waits for them, and re-layouts  2.65 us

profile of v6, /device:TPU:1, one launch (start us, length us, event | category | flops | bytes accessed | tf_op | source)
XLA Modules:
  0.0 88.8 jit_solution(3100017690648696340)
XLA Ops:
  0.0 86.1 %feti.1 = f32[1,1,1536,256]{3,2,1,0:T(8,128)} custom-call(bf16[1,1,1536,256]{3,2,1,0:T(8,128)(2,1)} %load_hbm.1, bf16[1,1,1536,1536]{3,2,1,0:T(8,128)(2,1)} %a_hbm.1, bf16[1,1,1536,1536]{3,2,1,0:T(8,128)(2,1)} %s_hbm.1, f32[1,1536]{1,0:T(1,128)} %bitcast.5, f32[1,16,1024]{2,1,0:T(8,128)} %cinv_hbm.1, s32[1,12]{1,0:T(1,128)} %bitcast.6, s32[1,12]{1,0:T(1,128)} %bitcast.7, ...), custom_call_target="tpu_custom_call" | custom-call | tf_op jit(solution)/shard_map/feti/pallas_call | solution.py:613
  86.2 2.7 %copy.11 = f32[1,1,1536,256]{3,2,1,0:T(8,128)} copy(f32[1,1,1536,256]{3,2,1,0:T(8,128)} %feti.1) | data formatting | bytes 3145728
